TPU v7x, 128 devices: a whole 4x4x4 slice. The times are simulated.
128 devices in a mesh: depth: 4 (over z_hi, core), lat: 32 (over z_lo, x, y).
Axes of the slice: x: 4, y: 4, z: 4 (z_hi: 2, z_lo: 2; z = z_hi * 2 + z_lo), core: 2. Of those that a mesh axis runs over, the one named last changes fastest.
Arguments:
- source_field: float32 [2, 4, 1024, 1024], P(None, None, 'lat'), may hold values from -9 to 9, as said below
- receiver_field: float32 [2, 4, 1024, 1024], P(None, None, 'lat'), may hold values from -9 to 9, as said below
- zone_index: int32 [16, 1024, 1024], P('depth', 'lat'), may hold values from 0 to 2
- blend_weight: int32 [16, 1024, 1024], P('depth', 'lat'), may hold values from 0 to 16
- ref_velocity: float32 [4], replicated, may hold values from 1500 to 4500
- frequencies: int32 [4], replicated, may hold values from 5 to 40
Outputs:
- migrated_image: float32 [16, 1024, 1024], P('depth', 'lat')
Inputs may be any that keep to these rules, and one draw needn't show every extreme that they name: `source_field`: surface wavefields of order one. `receiver_field`: recorded wavefields of order one.
All inputs are finite; a program needn't handle non-finite values.
Results may differ from a plain program's by a relative error of at most 0.0003.
Values sent between devices are 32-bit elements; how exact they have to be, the bound alone decides.
A program may use at most 64 MiB of HBM per device.

v0:
```python
import math

import jax
import jax.numpy as jnp
from jax import lax
from jax.sharding import PartitionSpec as P

HALF = 7
BLEND = 16


cell_width = 5.0
depth_step = 10.0
taper_width = 16.0


def padded_2(block, sides, width):
    for axis, dim in sides:
        count = lax.axis_size(axis)
        forward = [(i, i + 1) for i in range(count - 1)]
        backward = [(target, source) for source, target in forward]
        low = lax.ppermute(
            lax.slice_in_dim(block, block.shape[dim] - width, None, axis=dim), axis, forward
        )
        high = lax.ppermute(lax.slice_in_dim(block, 0, width, axis=dim), axis, backward)
        block = jnp.concatenate([low, block, high], axis=dim)
    return block


def sent_together(arrays, axis, dim, along):
    both = jnp.concatenate(arrays, axis=along)
    filled, at, done = (lax.all_gather(both, axis, axis=dim, tiled=True), 0, [])
    for a in arrays:
        done.append(lax.slice_in_dim(filled, at, at + a.shape[along], axis=along))
        at += a.shape[along]
    return tuple(done)


def in_blocks(value, dim, peers):
    before, after = (value.shape[:dim], value.shape[dim + 1 :])
    return jnp.moveaxis(value.reshape(*before, peers, -1, *after), dim, 0)


def sent_and_summed(value, axis, dim):
    blocks = in_blocks(value, dim, lax.axis_size(axis))
    arrived = lax.all_to_all(blocks, axis, split_axis=0, concat_axis=0, tiled=True)
    return arrived.sum(axis=0)


def kernels(frequencies, ref_velocity):
    offsets = jnp.arange(-HALF, HALF + 1, dtype=jnp.int32).astype(jnp.float32)
    wavenumber = 2.0 * math.pi * frequencies.astype(jnp.float32)[:, None] / ref_velocity[None, :]
    curvature = wavenumber * (cell_width * cell_width / (2.0 * depth_step))
    phase_turn = wavenumber * depth_step
    chirp_angle = curvature[:, :, None] * (offsets * offsets)[None, None, :]
    envelope = jnp.exp(-offsets * offsets / taper_width)
    raw_re = envelope * jnp.cos(chirp_angle)
    raw_im = envelope * jnp.sin(chirp_angle)
    magnitude = jnp.sqrt(jnp.sum(raw_re, axis=-1) ** 2 + jnp.sum(raw_im, axis=-1) ** 2)[:, :, None]
    return (raw_re / magnitude, raw_im / magnitude, jnp.cos(phase_turn), jnp.sin(phase_turn))


def convolve_rows(real, imag, tap_re, tap_im):
    length = real.shape[0] - 2 * HALF
    out_re = jnp.zeros((tap_re.shape[0], length, real.shape[1]), jnp.float32)
    out_im = jnp.zeros((tap_re.shape[0], length, real.shape[1]), jnp.float32)
    for offset in range(2 * HALF + 1):
        part_re = real[offset : offset + length][None]
        part_im = imag[offset : offset + length][None]
        coef_re = tap_re[:, offset][:, None, None]
        coef_im = tap_im[:, offset][:, None, None]
        out_re = out_re + coef_re * part_re - coef_im * part_im
        out_im = out_im + coef_re * part_im + coef_im * part_re
    return (out_re, out_im)


def convolve_cols(real, imag, tap_re, tap_im):
    length = real.shape[2] - 2 * HALF
    out_re = jnp.zeros(real.shape[:2] + (length,), jnp.float32)
    out_im = jnp.zeros(real.shape[:2] + (length,), jnp.float32)
    for offset in range(2 * HALF + 1):
        part_re = real[:, :, offset : offset + length]
        part_im = imag[:, :, offset : offset + length]
        coef_re = tap_re[:, offset][:, None, None]
        coef_im = tap_im[:, offset][:, None, None]
        out_re = out_re + coef_re * part_re - coef_im * part_im
        out_im = out_im + coef_re * part_im + coef_im * part_re
    return (out_re, out_im)


def advance(pad_re, pad_im, tap_re, tap_im, turn_cos, turn_sin, zone_level, weight_level):
    rows_re, rows_im = convolve_rows(pad_re, pad_im, tap_re, tap_im)
    widths = ((0, 0), (0, 0), (HALF, HALF))
    both_re, both_im = convolve_cols(
        jnp.pad(rows_re, widths), jnp.pad(rows_im, widths), tap_re, tap_im
    )
    phased_re = both_re * turn_cos[:, None, None] - both_im * turn_sin[:, None, None]
    phased_im = both_re * turn_sin[:, None, None] + both_im * turn_cos[:, None, None]
    reference_ids = jnp.arange(tap_re.shape[0], dtype=jnp.int32)[:, None, None]
    weights = jnp.where(reference_ids == zone_level[None], 1.0 - weight_level[None], 0.0)
    weights = weights + jnp.where(reference_ids == zone_level[None] + 1, weight_level[None], 0.0)
    return (jnp.sum(weights * phased_re, axis=0), jnp.sum(weights * phased_im, axis=0))


def local(source_field, receiver_field, zone_index, blend_weight, ref_velocity, frequencies):
    tap_re, tap_im, turn_cos, turn_sin = kernels(frequencies, ref_velocity)
    group_index = lax.axis_index("depth")
    groups = lax.axis_size("depth")
    freq_count = source_field.shape[1]
    surface = jnp.stack([source_field[0], source_field[1], receiver_field[0], receiver_field[1]])

    def single_step(padded, which, zone_level, weight_level):
        source_re, source_im = advance(
            padded[0],
            padded[1],
            tap_re[which],
            tap_im[which],
            turn_cos[which],
            turn_sin[which],
            zone_level,
            weight_level,
        )
        receiver_re, receiver_im = advance(
            padded[2],
            padded[3],
            tap_re[which],
            -tap_im[which],
            turn_cos[which],
            -turn_sin[which],
            zone_level,
            weight_level,
        )
        return jnp.stack([source_re, source_im, receiver_re, receiver_im])

    per_group = freq_count // groups
    first = group_index * per_group
    chosen_block = first + jnp.arange(per_group, dtype=jnp.int32)
    block_fields = lax.dynamic_slice_in_dim(surface, first, per_group, 1)
    zone_whole, blend_whole = sent_together((zone_index, blend_weight), "depth", 0, 1)

    def each_level(current, tables):
        zone_level, weight_level = tables
        padded = padded_2(current, (("lat", 2),), HALF)
        stepped = jax.vmap(single_step, in_axes=(1, 0, None, None), out_axes=1)(
            padded, chosen_block, zone_level, weight_level
        )
        return (stepped, stepped[0] * stepped[2] + stepped[1] * stepped[3])

    _, pieces = lax.scan(
        each_level, block_fields, (zone_whole, blend_whole.astype(jnp.float32) / BLEND)
    )
    migrated = sent_and_summed(jnp.sum(pieces, axis=1), "depth", 0)
    return migrated / freq_count


def solution(mesh):
    in_specs = (
        P(None, None, "lat", None),
        P(None, None, "lat", None),
        P("depth", "lat", None),
        P("depth", "lat", None),
        P(),
        P(),
    )
    out_specs = P("depth", "lat", None)
    return jax.shard_map(local, mesh=mesh, in_specs=in_specs, out_specs=out_specs, check_vma=False)
```

profile of v0, /device:TPU:97, one launch (start us, length us, event | category | flops | bytes accessed | tf_op | source)
XLA Modules:
  0.0 724.3 jit_solution(1033196603382220418)
XLA Ops:
  11.4 36.2 %all-gather.2.cloned.1.call-done = s32[16,64,1024]{2,1,0:T(8,128)} async-done(((s32[4,64,1024]{2,1,0:T(8,128)}), s32[16,64,1024]{2,1,0:T(8,128)}) %all-gather.2.cloned.1.call-update) | async-done | bytes 4194320 | tf_op jit(solution)/shard_map/all_gather | solution.py:32
  52.6 623.0 %while.21 = (s32[]{:T(128)}, f32[4,1,32,1024]{3,2,1,0:T(8,128)S(1)}, f32[16,1,32,1024]{3,2,1,0:T(8,128)}, s32[16,32,1024]{2,1,0:T(8,128)S(1)}, f32[16,32,1024]{2...) while((s32[]{:T(128)}, ...), condition=%wide.region_7.8_spmd, body=%wide.region_2.7_spmd.sunk | while | flops 65945600 | bytes 43588636 | solution.py:149
  53.2 5.8 collective-permute-start
  65.0 4.7 collective-permute-done.1
  77.5 16.0 %multiply_reduce_fusion.5 = (f32[32,1024]{1,0:T(8,128)S(1)}, f32[32,1024]{1,0:T(8,128)S(1)}, f32[32,1024]{1,0:T(8,128)S(1)}, f32[32,1024]{1,0:T(8,128)S(1)}) fusion(f32[4]{0:T(128)S(1)} %bitcast.246, f32[4]{0:T(128)S(1)} %bitcast.247, f32[32,1024]{1,0:T(8,128)S(1)} %get-tuple-element.689, s32[32,1024]{1,0:T(8,128)S(1)} %get-tuple-element.690, ...), kind=kLoop, calls=%fused_computation.65.clone.1 | loop fusion | flops 34078720 | bytes 3146496 | tf_op jit(solution)/shard_map/while/body/eval_jaxpr/vmap()/reduce_sum | solution.py:102
  115.7 16.0 %multiply_reduce_fusion.5 = (f32[32,1024]{1,0:T(8,128)S(1)}, f32[32,1024]{1,0:T(8,128)S(1)}, f32[32,1024]{1,0:T(8,128)S(1)}, f32[32,1024]{1,0:T(8,128)S(1)}) fusion(f32[4]{0:T(128)S(1)} %bitcast.246, f32[4]{0:T(128)S(1)} %bitcast.247, f32[32,1024]{1,0:T(8,128)S(1)} %get-tuple-element.689, s32[32,1024]{1,0:T(8,128)S(1)} %get-tuple-element.690, ...), kind=kLoop, calls=%fused_computation.65.clone.1 | loop fusion | flops 34078720 | bytes 3146496 | tf_op jit(solution)/shard_map/while/body/eval_jaxpr/vmap()/reduce_sum | solution.py:102
  142.5 4.0 collective-permute-done.1
  154.4 16.0 %multiply_reduce_fusion.5 = (f32[32,1024]{1,0:T(8,128)S(1)}, f32[32,1024]{1,0:T(8,128)S(1)}, f32[32,1024]{1,0:T(8,128)S(1)}, f32[32,1024]{1,0:T(8,128)S(1)}) fusion(f32[4]{0:T(128)S(1)} %bitcast.246, f32[4]{0:T(128)S(1)} %bitcast.247, f32[32,1024]{1,0:T(8,128)S(1)} %get-tuple-element.689, s32[32,1024]{1,0:T(8,128)S(1)} %get-tuple-element.690, ...), kind=kLoop, calls=%fused_computation.65.clone.1 | loop fusion | flops 34078720 | bytes 3146496 | tf_op jit(solution)/shard_map/while/body/eval_jaxpr/vmap()/reduce_sum | solution.py:102
  181.3 4.0 collective-permute-done.1
  193.2 16.0 %multiply_reduce_fusion.5 = (f32[32,1024]{1,0:T(8,128)S(1)}, f32[32,1024]{1,0:T(8,128)S(1)}, f32[32,1024]{1,0:T(8,128)S(1)}, f32[32,1024]{1,0:T(8,128)S(1)}) fusion(f32[4]{0:T(128)S(1)} %bitcast.246, f32[4]{0:T(128)S(1)} %bitcast.247, f32[32,1024]{1,0:T(8,128)S(1)} %get-tuple-element.689, s32[32,1024]{1,0:T(8,128)S(1)} %get-tuple-element.690, ...), kind=kLoop, calls=%fused_computation.65.clone.1 | loop fusion | flops 34078720 | bytes 3146496 | tf_op jit(solution)/shard_map/while/body/eval_jaxpr/vmap()/reduce_sum | solution.py:102
  232.0 16.0 %multiply_reduce_fusion.5 = (f32[32,1024]{1,0:T(8,128)S(1)}, f32[32,1024]{1,0:T(8,128)S(1)}, f32[32,1024]{1,0:T(8,128)S(1)}, f32[32,1024]{1,0:T(8,128)S(1)}) fusion(f32[4]{0:T(128)S(1)} %bitcast.246, f32[4]{0:T(128)S(1)} %bitcast.247, f32[32,1024]{1,0:T(8,128)S(1)} %get-tuple-element.689, s32[32,1024]{1,0:T(8,128)S(1)} %get-tuple-element.690, ...), kind=kLoop, calls=%fused_computation.65.clone.1 | loop fusion | flops 34078720 | bytes 3146496 | tf_op jit(solution)/shard_map/while/body/eval_jaxpr/vmap()/reduce_sum | solution.py:102
  270.8 16.0 %multiply_reduce_fusion.5 = (f32[32,1024]{1,0:T(8,128)S(1)}, f32[32,1024]{1,0:T(8,128)S(1)}, f32[32,1024]{1,0:T(8,128)S(1)}, f32[32,1024]{1,0:T(8,128)S(1)}) fusion(f32[4]{0:T(128)S(1)} %bitcast.246, f32[4]{0:T(128)S(1)} %bitcast.247, f32[32,1024]{1,0:T(8,128)S(1)} %get-tuple-element.689, s32[32,1024]{1,0:T(8,128)S(1)} %get-tuple-element.690, ...), kind=kLoop, calls=%fused_computation.65.clone.1 | loop fusion | flops 34078720 | bytes 3146496 | tf_op jit(solution)/shard_map/while/body/eval_jaxpr/vmap()/reduce_sum | solution.py:102
  309.6 16.0 %multiply_reduce_fusion.5 = (f32[32,1024]{1,0:T(8,128)S(1)}, f32[32,1024]{1,0:T(8,128)S(1)}, f32[32,1024]{1,0:T(8,128)S(1)}, f32[32,1024]{1,0:T(8,128)S(1)}) fusion(f32[4]{0:T(128)S(1)} %bitcast.246, f32[4]{0:T(128)S(1)} %bitcast.247, f32[32,1024]{1,0:T(8,128)S(1)} %get-tuple-element.689, s32[32,1024]{1,0:T(8,128)S(1)} %get-tuple-element.690, ...), kind=kLoop, calls=%fused_computation.65.clone.1 | loop fusion | flops 34078720 | bytes 3146496 | tf_op jit(solution)/shard_map/while/body/eval_jaxpr/vmap()/reduce_sum | solution.py:102
  348.4 16.0 %multiply_reduce_fusion.5 = (f32[32,1024]{1,0:T(8,128)S(1)}, f32[32,1024]{1,0:T(8,128)S(1)}, f32[32,1024]{1,0:T(8,128)S(1)}, f32[32,1024]{1,0:T(8,128)S(1)}) fusion(f32[4]{0:T(128)S(1)} %bitcast.246, f32[4]{0:T(128)S(1)} %bitcast.247, f32[32,1024]{1,0:T(8,128)S(1)} %get-tuple-element.689, s32[32,1024]{1,0:T(8,128)S(1)} %get-tuple-element.690, ...), kind=kLoop, calls=%fused_computation.65.clone.1 | loop fusion | flops 34078720 | bytes 3146496 | tf_op jit(solution)/shard_map/while/body/eval_jaxpr/vmap()/reduce_sum | solution.py:102
  387.2 16.0 %multiply_reduce_fusion.5 = (f32[32,1024]{1,0:T(8,128)S(1)}, f32[32,1024]{1,0:T(8,128)S(1)}, f32[32,1024]{1,0:T(8,128)S(1)}, f32[32,1024]{1,0:T(8,128)S(1)}) fusion(f32[4]{0:T(128)S(1)} %bitcast.246, f32[4]{0:T(128)S(1)} %bitcast.247, f32[32,1024]{1,0:T(8,128)S(1)} %get-tuple-element.689, s32[32,1024]{1,0:T(8,128)S(1)} %get-tuple-element.690, ...), kind=kLoop, calls=%fused_computation.65.clone.1 | loop fusion | flops 34078720 | bytes 3146496 | tf_op jit(solution)/shard_map/while/body/eval_jaxpr/vmap()/reduce_sum | solution.py:102
  426.0 16.0 %multiply_reduce_fusion.5 = (f32[32,1024]{1,0:T(8,128)S(1)}, f32[32,1024]{1,0:T(8,128)S(1)}, f32[32,1024]{1,0:T(8,128)S(1)}, f32[32,1024]{1,0:T(8,128)S(1)}) fusion(f32[4]{0:T(128)S(1)} %bitcast.246, f32[4]{0:T(128)S(1)} %bitcast.247, f32[32,1024]{1,0:T(8,128)S(1)} %get-tuple-element.689, s32[32,1024]{1,0:T(8,128)S(1)} %get-tuple-element.690, ...), kind=kLoop, calls=%fused_computation.65.clone.1 | loop fusion | flops 34078720 | bytes 3146496 | tf_op jit(solution)/shard_map/while/body/eval_jaxpr/vmap()/reduce_sum | solution.py:102
  464.8 16.0 %multiply_reduce_fusion.5 = (f32[32,1024]{1,0:T(8,128)S(1)}, f32[32,1024]{1,0:T(8,128)S(1)}, f32[32,1024]{1,0:T(8,128)S(1)}, f32[32,1024]{1,0:T(8,128)S(1)}) fusion(f32[4]{0:T(128)S(1)} %bitcast.246, f32[4]{0:T(128)S(1)} %bitcast.247, f32[32,1024]{1,0:T(8,128)S(1)} %get-tuple-element.689, s32[32,1024]{1,0:T(8,128)S(1)} %get-tuple-element.690, ...), kind=kLoop, calls=%fused_computation.65.clone.1 | loop fusion | flops 34078720 | bytes 3146496 | tf_op jit(solution)/shard_map/while/body/eval_jaxpr/vmap()/reduce_sum | solution.py:102
  503.6 16.0 %multiply_reduce_fusion.5 = (f32[32,1024]{1,0:T(8,128)S(1)}, f32[32,1024]{1,0:T(8,128)S(1)}, f32[32,1024]{1,0:T(8,128)S(1)}, f32[32,1024]{1,0:T(8,128)S(1)}) fusion(f32[4]{0:T(128)S(1)} %bitcast.246, f32[4]{0:T(128)S(1)} %bitcast.247, f32[32,1024]{1,0:T(8,128)S(1)} %get-tuple-element.689, s32[32,1024]{1,0:T(8,128)S(1)} %get-tuple-element.690, ...), kind=kLoop, calls=%fused_computation.65.clone.1 | loop fusion | flops 34078720 | bytes 3146496 | tf_op jit(solution)/shard_map/while/body/eval_jaxpr/vmap()/reduce_sum | solution.py:102
  542.3 16.0 %multiply_reduce_fusion.5 = (f32[32,1024]{1,0:T(8,128)S(1)}, f32[32,1024]{1,0:T(8,128)S(1)}, f32[32,1024]{1,0:T(8,128)S(1)}, f32[32,1024]{1,0:T(8,128)S(1)}) fusion(f32[4]{0:T(128)S(1)} %bitcast.246, f32[4]{0:T(128)S(1)} %bitcast.247, f32[32,1024]{1,0:T(8,128)S(1)} %get-tuple-element.689, s32[32,1024]{1,0:T(8,128)S(1)} %get-tuple-element.690, ...), kind=kLoop, calls=%fused_computation.65.clone.1 | loop fusion | flops 34078720 | bytes 3146496 | tf_op jit(solution)/shard_map/while/body/eval_jaxpr/vmap()/reduce_sum | solution.py:102
  581.1 16.0 %multiply_reduce_fusion.5 = (f32[32,1024]{1,0:T(8,128)S(1)}, f32[32,1024]{1,0:T(8,128)S(1)}, f32[32,1024]{1,0:T(8,128)S(1)}, f32[32,1024]{1,0:T(8,128)S(1)}) fusion(f32[4]{0:T(128)S(1)} %bitcast.246, f32[4]{0:T(128)S(1)} %bitcast.247, f32[32,1024]{1,0:T(8,128)S(1)} %get-tuple-element.689, s32[32,1024]{1,0:T(8,128)S(1)} %get-tuple-element.690, ...), kind=kLoop, calls=%fused_computation.65.clone.1 | loop fusion | flops 34078720 | bytes 3146496 | tf_op jit(solution)/shard_map/while/body/eval_jaxpr/vmap()/reduce_sum | solution.py:102
  619.9 16.0 %multiply_reduce_fusion.5 = (f32[32,1024]{1,0:T(8,128)S(1)}, f32[32,1024]{1,0:T(8,128)S(1)}, f32[32,1024]{1,0:T(8,128)S(1)}, f32[32,1024]{1,0:T(8,128)S(1)}) fusion(f32[4]{0:T(128)S(1)} %bitcast.246, f32[4]{0:T(128)S(1)} %bitcast.247, f32[32,1024]{1,0:T(8,128)S(1)} %get-tuple-element.689, s32[32,1024]{1,0:T(8,128)S(1)} %get-tuple-element.690, ...), kind=kLoop, calls=%fused_computation.65.clone.1 | loop fusion | flops 34078720 | bytes 3146496 | tf_op jit(solution)/shard_map/while/body/eval_jaxpr/vmap()/reduce_sum | solution.py:102
  646.8 4.1 collective-permute-done.1
  658.8 16.0 %multiply_reduce_fusion.5 = (f32[32,1024]{1,0:T(8,128)S(1)}, f32[32,1024]{1,0:T(8,128)S(1)}, f32[32,1024]{1,0:T(8,128)S(1)}, f32[32,1024]{1,0:T(8,128)S(1)}) fusion(f32[4]{0:T(128)S(1)} %bitcast.246, f32[4]{0:T(128)S(1)} %bitcast.247, f32[32,1024]{1,0:T(8,128)S(1)} %get-tuple-element.689, s32[32,1024]{1,0:T(8,128)S(1)} %get-tuple-element.690, ...), kind=kLoop, calls=%fused_computation.65.clone.1 | loop fusion | flops 34078720 | bytes 3146496 | tf_op jit(solution)/shard_map/while/body/eval_jaxpr/vmap()/reduce_sum | solution.py:102
  675.5 40.9 %all_to_all.5 = f32[4,4,32,1024]{3,2,1,0:T(8,128)S(1)} all-to-all(f32[4,4,32,1024]{3,2,1,0:T(8,128)} %bitcast.244), channel_id=1, replica_groups=mesh['depth'=4,'lat'=32] {'depth'}, dimensions={0} | all-to-all | bytes 4194304 | tf_op jit(solution)/shard_map/all_to_all | solution.py:46
  (1368 shorter events, 349.0 us)
Async XLA Ops:
  6.5 41.1 %all-gather.2.cloned.1.call-start = ((), (), s32[]{:S(2)}) async-start(), calls=%async_computation.1 | async-start | bytes 5242880 | tf_op jit(solution)/shard_map/all_gather | solution.py:32
  53.2 11.7 %collective-permute-start = (f32[4,1,7,1024]{3,2,1,0:T(8,128)}, f32[4,1,7,1024]{3,2,1,0:T(8,128)S(1)}, u32[]{:S(2)}, u32[]{:S(2)}) collective-permute-start(f32[4,1,7,1024]{3,2,1,0:T(8,128)} %get-tuple-element.707), channel_id=1, source_target_pairs={{1,0},{2,1},{3,2},{4,3},{5,4},{6,5},{7,6},{8,7},{9,8},{10,9},{11,1... | collective-permute-start | bytes 344072 | tf_op jit(solution)/shard_map/while/body/eval_jaxpr/ppermute | solution.py:25
  59.0 10.6 %collective-permute-start.1 = (f32[4,1,7,1024]{3,2,1,0:T(8,128)S(1)}, f32[4,1,7,1024]{3,2,1,0:T(8,128)S(1)}, u32[]{:S(2)}, u32[]{:S(2)}) collective-permute-start(f32[4,1,7,1024]{3,2,1,0:T(8,128)S(1)} %get-tuple-element.708), channel_id=1, source_target_pairs={{0,1},{1,2},{2,3},{3,4},{4,5},{5,6},{6,7},{7,8},{8,9},{9,10},{10,1... | collective-permute-start | bytes 344072 | tf_op jit(solution)/shard_map/while/body/eval_jaxpr/ppermute | solution.py:22
  97.8 9.9 %collective-permute-start.1 = (f32[4,1,7,1024]{3,2,1,0:T(8,128)S(1)}, f32[4,1,7,1024]{3,2,1,0:T(8,128)S(1)}, u32[]{:S(2)}, u32[]{:S(2)}) collective-permute-start(f32[4,1,7,1024]{3,2,1,0:T(8,128)S(1)} %get-tuple-element.708), channel_id=1, source_target_pairs={{0,1},{1,2},{2,3},{3,4},{4,5},{5,6},{6,7},{7,8},{8,9},{9,10},{10,1... | collective-permute-start | bytes 344072 | tf_op jit(solution)/shard_map/while/body/eval_jaxpr/ppermute | solution.py:22
  136.6 9.9 %collective-permute-start.1 = (f32[4,1,7,1024]{3,2,1,0:T(8,128)S(1)}, f32[4,1,7,1024]{3,2,1,0:T(8,128)S(1)}, u32[]{:S(2)}, u32[]{:S(2)}) collective-permute-start(f32[4,1,7,1024]{3,2,1,0:T(8,128)S(1)} %get-tuple-element.708), channel_id=1, source_target_pairs={{0,1},{1,2},{2,3},{3,4},{4,5},{5,6},{6,7},{7,8},{8,9},{9,10},{10,1... | collective-permute-start | bytes 344072 | tf_op jit(solution)/shard_map/while/body/eval_jaxpr/ppermute | solution.py:22
  171.8 9.5 %collective-permute-start = (f32[4,1,7,1024]{3,2,1,0:T(8,128)}, f32[4,1,7,1024]{3,2,1,0:T(8,128)S(1)}, u32[]{:S(2)}, u32[]{:S(2)}) collective-permute-start(f32[4,1,7,1024]{3,2,1,0:T(8,128)} %get-tuple-element.707), channel_id=1, source_target_pairs={{1,0},{2,1},{3,2},{4,3},{5,4},{6,5},{7,6},{8,7},{9,8},{10,9},{11,1... | collective-permute-start | bytes 344072 | tf_op jit(solution)/shard_map/while/body/eval_jaxpr/ppermute | solution.py:25
  175.4 9.9 %collective-permute-start.1 = (f32[4,1,7,1024]{3,2,1,0:T(8,128)S(1)}, f32[4,1,7,1024]{3,2,1,0:T(8,128)S(1)}, u32[]{:S(2)}, u32[]{:S(2)}) collective-permute-start(f32[4,1,7,1024]{3,2,1,0:T(8,128)S(1)} %get-tuple-element.708), channel_id=1, source_target_pairs={{0,1},{1,2},{2,3},{3,4},{4,5},{5,6},{6,7},{7,8},{8,9},{9,10},{10,1... | collective-permute-start | bytes 344072 | tf_op jit(solution)/shard_map/while/body/eval_jaxpr/ppermute | solution.py:22
  214.2 9.9 %collective-permute-start.1 = (f32[4,1,7,1024]{3,2,1,0:T(8,128)S(1)}, f32[4,1,7,1024]{3,2,1,0:T(8,128)S(1)}, u32[]{:S(2)}, u32[]{:S(2)}) collective-permute-start(f32[4,1,7,1024]{3,2,1,0:T(8,128)S(1)} %get-tuple-element.708), channel_id=1, source_target_pairs={{0,1},{1,2},{2,3},{3,4},{4,5},{5,6},{6,7},{7,8},{8,9},{9,10},{10,1... | collective-permute-start | bytes 344072 | tf_op jit(solution)/shard_map/while/body/eval_jaxpr/ppermute | solution.py:22
  253.0 9.9 %collective-permute-start.1 = (f32[4,1,7,1024]{3,2,1,0:T(8,128)S(1)}, f32[4,1,7,1024]{3,2,1,0:T(8,128)S(1)}, u32[]{:S(2)}, u32[]{:S(2)}) collective-permute-start(f32[4,1,7,1024]{3,2,1,0:T(8,128)S(1)} %get-tuple-element.708), channel_id=1, source_target_pairs={{0,1},{1,2},{2,3},{3,4},{4,5},{5,6},{6,7},{7,8},{8,9},{9,10},{10,1... | collective-permute-start | bytes 344072 | tf_op jit(solution)/shard_map/while/body/eval_jaxpr/ppermute | solution.py:22
  291.8 9.9 %collective-permute-start.1 = (f32[4,1,7,1024]{3,2,1,0:T(8,128)S(1)}, f32[4,1,7,1024]{3,2,1,0:T(8,128)S(1)}, u32[]{:S(2)}, u32[]{:S(2)}) collective-permute-start(f32[4,1,7,1024]{3,2,1,0:T(8,128)S(1)} %get-tuple-element.708), channel_id=1, source_target_pairs={{0,1},{1,2},{2,3},{3,4},{4,5},{5,6},{6,7},{7,8},{8,9},{9,10},{10,1... | collective-permute-start | bytes 344072 | tf_op jit(solution)/shard_map/while/body/eval_jaxpr/ppermute | solution.py:22
  327.0 9.5 %collective-permute-start = (f32[4,1,7,1024]{3,2,1,0:T(8,128)}, f32[4,1,7,1024]{3,2,1,0:T(8,128)S(1)}, u32[]{:S(2)}, u32[]{:S(2)}) collective-permute-start(f32[4,1,7,1024]{3,2,1,0:T(8,128)} %get-tuple-element.707), channel_id=1, source_target_pairs={{1,0},{2,1},{3,2},{4,3},{5,4},{6,5},{7,6},{8,7},{9,8},{10,9},{11,1... | collective-permute-start | bytes 344072 | tf_op jit(solution)/shard_map/while/body/eval_jaxpr/ppermute | solution.py:25
  330.6 9.9 %collective-permute-start.1 = (f32[4,1,7,1024]{3,2,1,0:T(8,128)S(1)}, f32[4,1,7,1024]{3,2,1,0:T(8,128)S(1)}, u32[]{:S(2)}, u32[]{:S(2)}) collective-permute-start(f32[4,1,7,1024]{3,2,1,0:T(8,128)S(1)} %get-tuple-element.708), channel_id=1, source_target_pairs={{0,1},{1,2},{2,3},{3,4},{4,5},{5,6},{6,7},{7,8},{8,9},{9,10},{10,1... | collective-permute-start | bytes 344072 | tf_op jit(solution)/shard_map/while/body/eval_jaxpr/ppermute | solution.py:22
  365.8 9.5 %collective-permute-start = (f32[4,1,7,1024]{3,2,1,0:T(8,128)}, f32[4,1,7,1024]{3,2,1,0:T(8,128)S(1)}, u32[]{:S(2)}, u32[]{:S(2)}) collective-permute-start(f32[4,1,7,1024]{3,2,1,0:T(8,128)} %get-tuple-element.707), channel_id=1, source_target_pairs={{1,0},{2,1},{3,2},{4,3},{5,4},{6,5},{7,6},{8,7},{9,8},{10,9},{11,1... | collective-permute-start | bytes 344072 | tf_op jit(solution)/shard_map/while/body/eval_jaxpr/ppermute | solution.py:25
  369.4 9.9 %collective-permute-start.1 = (f32[4,1,7,1024]{3,2,1,0:T(8,128)S(1)}, f32[4,1,7,1024]{3,2,1,0:T(8,128)S(1)}, u32[]{:S(2)}, u32[]{:S(2)}) collective-permute-start(f32[4,1,7,1024]{3,2,1,0:T(8,128)S(1)} %get-tuple-element.708), channel_id=1, source_target_pairs={{0,1},{1,2},{2,3},{3,4},{4,5},{5,6},{6,7},{7,8},{8,9},{9,10},{10,1... | collective-permute-start | bytes 344072 | tf_op jit(solution)/shard_map/while/body/eval_jaxpr/ppermute | solution.py:22
  408.2 9.9 %collective-permute-start.1 = (f32[4,1,7,1024]{3,2,1,0:T(8,128)S(1)}, f32[4,1,7,1024]{3,2,1,0:T(8,128)S(1)}, u32[]{:S(2)}, u32[]{:S(2)}) collective-permute-start(f32[4,1,7,1024]{3,2,1,0:T(8,128)S(1)} %get-tuple-element.708), channel_id=1, source_target_pairs={{0,1},{1,2},{2,3},{3,4},{4,5},{5,6},{6,7},{7,8},{8,9},{9,10},{10,1... | collective-permute-start | bytes 344072 | tf_op jit(solution)/shard_map/while/body/eval_jaxpr/ppermute | solution.py:22
  443.4 9.5 %collective-permute-start = (f32[4,1,7,1024]{3,2,1,0:T(8,128)}, f32[4,1,7,1024]{3,2,1,0:T(8,128)S(1)}, u32[]{:S(2)}, u32[]{:S(2)}) collective-permute-start(f32[4,1,7,1024]{3,2,1,0:T(8,128)} %get-tuple-element.707), channel_id=1, source_target_pairs={{1,0},{2,1},{3,2},{4,3},{5,4},{6,5},{7,6},{8,7},{9,8},{10,9},{11,1... | collective-permute-start | bytes 344072 | tf_op jit(solution)/shard_map/while/body/eval_jaxpr/ppermute | solution.py:25
  446.9 9.9 %collective-permute-start.1 = (f32[4,1,7,1024]{3,2,1,0:T(8,128)S(1)}, f32[4,1,7,1024]{3,2,1,0:T(8,128)S(1)}, u32[]{:S(2)}, u32[]{:S(2)}) collective-permute-start(f32[4,1,7,1024]{3,2,1,0:T(8,128)S(1)} %get-tuple-element.708), channel_id=1, source_target_pairs={{0,1},{1,2},{2,3},{3,4},{4,5},{5,6},{6,7},{7,8},{8,9},{9,10},{10,1... | collective-permute-start | bytes 344072 | tf_op jit(solution)/shard_map/while/body/eval_jaxpr/ppermute | solution.py:22
  482.2 9.5 %collective-permute-start = (f32[4,1,7,1024]{3,2,1,0:T(8,128)}, f32[4,1,7,1024]{3,2,1,0:T(8,128)S(1)}, u32[]{:S(2)}, u32[]{:S(2)}) collective-permute-start(f32[4,1,7,1024]{3,2,1,0:T(8,128)} %get-tuple-element.707), channel_id=1, source_target_pairs={{1,0},{2,1},{3,2},{4,3},{5,4},{6,5},{7,6},{8,7},{9,8},{10,9},{11,1... | collective-permute-start | bytes 344072 | tf_op jit(solution)/shard_map/while/body/eval_jaxpr/ppermute | solution.py:25
  485.7 9.9 %collective-permute-start.1 = (f32[4,1,7,1024]{3,2,1,0:T(8,128)S(1)}, f32[4,1,7,1024]{3,2,1,0:T(8,128)S(1)}, u32[]{:S(2)}, u32[]{:S(2)}) collective-permute-start(f32[4,1,7,1024]{3,2,1,0:T(8,128)S(1)} %get-tuple-element.708), channel_id=1, source_target_pairs={{0,1},{1,2},{2,3},{3,4},{4,5},{5,6},{6,7},{7,8},{8,9},{9,10},{10,1... | collective-permute-start | bytes 344072 | tf_op jit(solution)/shard_map/while/body/eval_jaxpr/ppermute | solution.py:22
  524.5 9.9 %collective-permute-start.1 = (f32[4,1,7,1024]{3,2,1,0:T(8,128)S(1)}, f32[4,1,7,1024]{3,2,1,0:T(8,128)S(1)}, u32[]{:S(2)}, u32[]{:S(2)}) collective-permute-start(f32[4,1,7,1024]{3,2,1,0:T(8,128)S(1)} %get-tuple-element.708), channel_id=1, source_target_pairs={{0,1},{1,2},{2,3},{3,4},{4,5},{5,6},{6,7},{7,8},{8,9},{9,10},{10,1... | collective-permute-start | bytes 344072 | tf_op jit(solution)/shard_map/while/body/eval_jaxpr/ppermute | solution.py:22
  563.3 9.9 %collective-permute-start.1 = (f32[4,1,7,1024]{3,2,1,0:T(8,128)S(1)}, f32[4,1,7,1024]{3,2,1,0:T(8,128)S(1)}, u32[]{:S(2)}, u32[]{:S(2)}) collective-permute-start(f32[4,1,7,1024]{3,2,1,0:T(8,128)S(1)} %get-tuple-element.708), channel_id=1, source_target_pairs={{0,1},{1,2},{2,3},{3,4},{4,5},{5,6},{6,7},{7,8},{8,9},{9,10},{10,1... | collective-permute-start | bytes 344072 | tf_op jit(solution)/shard_map/while/body/eval_jaxpr/ppermute | solution.py:22
  598.5 9.5 %collective-permute-start = (f32[4,1,7,1024]{3,2,1,0:T(8,128)}, f32[4,1,7,1024]{3,2,1,0:T(8,128)S(1)}, u32[]{:S(2)}, u32[]{:S(2)}) collective-permute-start(f32[4,1,7,1024]{3,2,1,0:T(8,128)} %get-tuple-element.707), channel_id=1, source_target_pairs={{1,0},{2,1},{3,2},{4,3},{5,4},{6,5},{7,6},{8,7},{9,8},{10,9},{11,1... | collective-permute-start | bytes 344072 | tf_op jit(solution)/shard_map/while/body/eval_jaxpr/ppermute | solution.py:25
  602.1 9.9 %collective-permute-start.1 = (f32[4,1,7,1024]{3,2,1,0:T(8,128)S(1)}, f32[4,1,7,1024]{3,2,1,0:T(8,128)S(1)}, u32[]{:S(2)}, u32[]{:S(2)}) collective-permute-start(f32[4,1,7,1024]{3,2,1,0:T(8,128)S(1)} %get-tuple-element.708), channel_id=1, source_target_pairs={{0,1},{1,2},{2,3},{3,4},{4,5},{5,6},{6,7},{7,8},{8,9},{9,10},{10,1... | collective-permute-start | bytes 344072 | tf_op jit(solution)/shard_map/while/body/eval_jaxpr/ppermute | solution.py:22
  640.9 10.0 %collective-permute-start.1 = (f32[4,1,7,1024]{3,2,1,0:T(8,128)S(1)}, f32[4,1,7,1024]{3,2,1,0:T(8,128)S(1)}, u32[]{:S(2)}, u32[]{:S(2)}) collective-permute-start(f32[4,1,7,1024]{3,2,1,0:T(8,128)S(1)} %get-tuple-element.708), channel_id=1, source_target_pairs={{0,1},{1,2},{2,3},{3,4},{4,5},{5,6},{6,7},{7,8},{8,9},{9,10},{10,1... | collective-permute-start | bytes 344072 | tf_op jit(solution)/shard_map/while/body/eval_jaxpr/ppermute | solution.py:22
  (510 other events, 473.4 us)
Sparse Core Ops, SparseCore 0:
  9.2 38.4 all-gather.1
where the time goes:
time: 729 us; the launch traced here: 724 us
  other arithmetic  389 us (53%)
  waiting for transfers between devices  101 us (14%)
  starting transfers between devices  89.8 us (12%)
  local copies, waits for them, and re-layouts  83.8 us (11%)
  blocking collectives  40.9 us (6%)
  between operations  13.5 us (2%)
    reduce_sum x16, other arithmetic, advance(): jnp.sum(weights * phased_re, axis=0)  255 us
    ppermute x16, waiting for transfers between devices, padded_2(): lax.ppermute(lax.slice_in_dim(block, block.shape[dim] - width, None, axis...  64.5 us
    ppermute x16, starting transfers between devices, padded_2(): lax.ppermute(lax.slice_in_dim(block, 0, width, axis=dim), axis, backward)  58.6 us
    add x32, other arithmetic, convolve_rows(): out_im = out_im + coef_re * part_im + coef_im * part_re  48.6 us
    sub x32, other arithmetic, convolve_rows(): out_re = out_re + coef_re * part_re - coef_im * part_im  48.5 us
    all_to_all x1, blocking collectives, sent_and_summed(): lax.all_to_all(blocks, axis, split_axis=0, concat_axis=0, tiled=True)  40.9 us
    mul x80, local copies, waits for them, and re-layouts, convolve_rows(): out_re = out_re + coef_re * part_re - coef_im * part_im  39.5 us
    all_gather x1, waiting for transfers between devices, sent_together(): filled, at, done = (lax.all_gather(both, axis, axis=dim, tiled=True), 0, [])  36.2 us
  transfers between devices with their start and end apart: 33, of which 17 were waited for; matrix products, arithmetic and copies ran while one was open for 9% of the time, Pallas kernels for 0%

commit v1 on v0

v1 whole, which is shorter than its diff:
```python
import functools
import math

import jax
import jax.numpy as jnp
from jax import lax
from jax.experimental import pallas as pl
from jax.experimental.pallas import tpu as pltpu
from jax.sharding import PartitionSpec as P

HALF = 7
BLEND = 16
LANES = 128
PAD = 128
STEP = LANES - 2 * HALF
HALO = 8
GROUP = 16

cell_width = 5.0
depth_step = 10.0
taper_width = 16.0


def kernels(frequency, ref_velocity):
    offsets = jnp.arange(0, HALF + 1, dtype=jnp.int32).astype(jnp.float32)
    wavenumber = 2.0 * math.pi * frequency.astype(jnp.float32) / ref_velocity
    curvature = wavenumber * (cell_width * cell_width / (2.0 * depth_step))
    phase_turn = wavenumber * depth_step
    chirp_angle = curvature[:, None] * (offsets * offsets)[None, :]
    envelope = jnp.exp(-offsets * offsets / taper_width)
    raw_re = envelope * jnp.cos(chirp_angle)
    raw_im = envelope * jnp.sin(chirp_angle)
    both = jnp.where(offsets == 0.0, 1.0, 2.0)
    magnitude = jnp.sqrt(
        jnp.sum(both * raw_re, axis=-1) ** 2 + jnp.sum(both * raw_im, axis=-1) ** 2
    )[:, None]
    return raw_re / magnitude, raw_im / magnitude, jnp.cos(phase_turn), jnp.sin(phase_turn)


def split(x):
    high = lax.reduce_precision(x, 8, 7)
    return high.astype(jnp.bfloat16), (x - high).astype(jnp.bfloat16)


def banded(taps, distance, keep):
    out = jnp.zeros((taps.shape[0],) + distance.shape, jnp.float32)
    for m in range(HALF + 1):
        out = jnp.where((distance == m) & keep, taps[:, m][:, None, None], out)
    return out


def matrices(frequency, ref_velocity):
    c_re, c_im, turn_cos, turn_sin = kernels(frequency, ref_velocity)
    refs = c_re.shape[0]
    r = jnp.arange(GROUP)[:, None]
    k = jnp.arange(2 * GROUP)[None, :]
    distance = jnp.abs(k - HALO - r)
    a_re, a_im = (banded(t, distance, True) for t in (c_re, c_im))
    x_mat = jnp.concatenate(
        [jnp.concatenate([a_re, -a_im], 2), jnp.concatenate([a_im, a_re], 2)], 1
    ).reshape(refs * 2 * GROUP, 4 * GROUP)
    x_high, x_low = split(x_mat)
    x_all = jnp.concatenate([x_high, x_high, x_low], 1)
    d_re = c_re * turn_cos[:, None] - c_im * turn_sin[:, None]
    d_im = c_re * turn_sin[:, None] + c_im * turn_cos[:, None]
    k = jnp.arange(LANES)[:, None]
    n = jnp.arange(LANES)[None, :]
    distance = jnp.abs(k - HALF - n)
    b_re, b_im = (banded(t, distance, n < STEP) for t in (d_re, d_im))
    y_mat = jnp.concatenate(
        [jnp.concatenate([b_re, b_im], 2), jnp.concatenate([-b_im, b_re], 2)], 1
    )
    y_high, y_low = split(y_mat)
    return x_all, jnp.concatenate([y_high, y_high, y_low], 1)


def two_parts(x):
    high = x.astype(jnp.bfloat16)
    return high, (x - high.astype(jnp.float32)).astype(jnp.bfloat16)


def body(
    lat_size, source, receiver, zone, blend, x_mat, y_mat,
    image, field, halo, xbuf, ybuf, load_sem, send_sem, recv_sem,
):
    levels = zone.shape[0]
    rows, cols = zone.shape[1:]
    refs = y_mat.shape[0]
    windows = -(-cols // STEP)
    lat = lax.axis_index("lat")
    chosen = lax.axis_index("depth")
    has_up = lat > 0
    has_down = lat < lat_size - 1
    inner = pl.ds(PAD, cols)

    loads = [
        pltpu.make_async_copy(
            ref.at[:, chosen], field.at[f, :, :, inner], load_sem.at[f]
        )
        for f, ref in enumerate((source, receiver))
    ]
    for load in loads:
        load.start()
    halo[...] = jnp.zeros_like(halo)
    for f in range(2):
        for c in range(2):
            field[f, c, :, 0:PAD] = jnp.zeros((rows, PAD), jnp.float32)
            field[f, c, :, PAD + cols :] = jnp.zeros((rows, PAD), jnp.float32)

    barrier = pltpu.get_barrier_semaphore()

    @pl.when(has_up)
    def _():
        pl.semaphore_signal(barrier, inc=1, device_id={"lat": lat - 1})

    @pl.when(has_down)
    def _():
        pl.semaphore_signal(barrier, inc=1, device_id={"lat": lat + 1})

    pl.semaphore_wait(barrier, has_up.astype(jnp.int32) + has_down.astype(jnp.int32))

    def to_up(f, slot):
        return pltpu.make_async_remote_copy(
            src_ref=field.at[f, :, pl.ds(0, HALO), inner],
            dst_ref=halo.at[slot, f, 1, :, :, inner],
            send_sem=send_sem.at[f, 0],
            recv_sem=recv_sem.at[slot, f, 1],
            device_id={"lat": lat - 1},
        )

    def to_down(f, slot):
        return pltpu.make_async_remote_copy(
            src_ref=field.at[f, :, pl.ds(rows - HALO, HALO), inner],
            dst_ref=halo.at[slot, f, 0, :, :, inner],
            send_sem=send_sem.at[f, 1],
            recv_sem=recv_sem.at[slot, f, 0],
            device_id={"lat": lat + 1},
        )

    def each_side(act_up, act_down):
        @pl.when(has_up)
        def _():
            act_up()

        @pl.when(has_down)
        def _():
            act_down()

    def send(f, slot):
        each_side(lambda: to_up(f, slot).start(), lambda: to_down(f, slot).start())

    def wait_sent(f, slot):
        each_side(lambda: to_up(f, slot).wait_send(), lambda: to_down(f, slot).wait_send())

    def wait_arrived(f, slot):
        each_side(lambda: to_down(f, slot).wait_recv(), lambda: to_up(f, slot).wait_recv())

    for f in range(2):
        loads[f].wait()
        if f == 1:
            field[1, 1] = -field[1, 1]
        send(f, 0)

    def level(z, carry):
        slot = lax.rem(z, 2)
        for f in range(2):
            wait_arrived(f, slot)
            for w in range(windows):
                at = pl.ds(PAD + w * STEP - HALF, LANES)
                parts = []
                for group in range(rows // GROUP):
                    column = []
                    for c in range(2):
                        first = group * GROUP - HALO
                        pieces = []
                        if first < 0:
                            pieces.append(halo[slot, f, 0, c, :, at])
                        low, high = max(first, 0), min(first + 2 * GROUP, rows)
                        pieces.append(field[f, c, low:high, at])
                        if first + 2 * GROUP > rows:
                            pieces.append(halo[slot, f, 1, c, :, at])
                        column.append(jnp.concatenate(pieces, 0))
                    parts.append(jnp.concatenate(column, 0))
                high, low = two_parts(jnp.concatenate(parts, 1))
                out = jnp.dot(
                    x_mat[...],
                    jnp.concatenate([high, low, high], 0),
                    preferred_element_type=jnp.float32,
                )
                for part, values in enumerate(two_parts(out)):
                    for j in range(refs):
                        for c in range(2):
                            for group in range(rows // GROUP):
                                top = (j * 2 + c) * GROUP
                                left = group * LANES
                                xbuf[
                                    j,
                                    w * rows + group * GROUP : w * rows + (group + 1) * GROUP,
                                    (part * 2 + c) * LANES : (part * 2 + c + 1) * LANES,
                                ] = values[top : top + GROUP, left : left + LANES]
            wait_sent(f, slot)
            for j in range(refs):
                ybuf[j] = jnp.dot(
                    jnp.concatenate([xbuf[j], xbuf[j, :, 0 : 2 * LANES]], 1),
                    y_mat[j],
                    preferred_element_type=jnp.float32,
                )
            for w in range(windows):
                width = min(STEP, cols - w * STEP)
                here = pl.ds(w * STEP, width)
                which = zone[z, :, here]
                upper = blend[z, :, here].astype(jnp.float32) * (1.0 / BLEND)
                lower = 1.0 - upper
                total = [jnp.zeros((rows, width), jnp.float32)] * 2
                for j in range(refs):
                    weight = jnp.where(which == j, lower, jnp.where(which == j - 1, upper, 0.0))
                    for c in range(2):
                        total[c] = total[c] + weight * (
                            ybuf[j, w * rows : (w + 1) * rows, c * LANES : c * LANES + width]
                        )
                for c in range(2):
                    field[f, c, :, pl.ds(PAD + w * STEP, width)] = total[c]

            @pl.when(z < levels - 1)
            def _():
                send(f, 1 - slot)

        image[z] = (
            field[0, 0, :, inner] * field[1, 0, :, inner]
            - field[0, 1, :, inner] * field[1, 1, :, inner]
        )
        return carry

    lax.fori_loop(0, levels, level, 0)


def migrate(lat_size, source, receiver, zone, blend, x_mat, y_mat):
    levels, rows, cols = zone.shape
    windows = -(-cols // STEP)
    refs = y_mat.shape[0]
    vmem = pl.BlockSpec(memory_space=pltpu.VMEM)
    hbm = pl.BlockSpec(memory_space=pl.ANY)
    wide = cols + 2 * PAD
    return pl.pallas_call(
        functools.partial(body, lat_size),
        out_shape=jax.ShapeDtypeStruct((levels, rows, cols), jnp.float32),
        in_specs=[hbm, hbm, vmem, vmem, vmem, vmem],
        out_specs=vmem,
        scratch_shapes=[
            pltpu.VMEM((2, 2, rows, wide), jnp.float32),
            pltpu.VMEM((2, 2, 2, 2, HALO, wide), jnp.float32),
            pltpu.VMEM((refs, windows * rows, 4 * LANES), jnp.bfloat16),
            pltpu.VMEM((refs, windows * rows, 2 * LANES), jnp.float32),
            pltpu.SemaphoreType.DMA((2,)),
            pltpu.SemaphoreType.DMA((2, 2)),
            pltpu.SemaphoreType.DMA((2, 2, 2)),
        ],
        compiler_params=pltpu.CompilerParams(
            collective_id=0, has_side_effects=True, vmem_limit_bytes=60 * 2**20
        ),
    )(source, receiver, zone, blend, x_mat, y_mat)


def local(lat_size, source_field, receiver_field, zone_index, blend_weight, ref_velocity, frequencies):
    group_index = lax.axis_index("depth")
    groups = lax.axis_size("depth")
    freq_count = source_field.shape[1]
    frequency = lax.dynamic_index_in_dim(frequencies, group_index, keepdims=False)
    x_mat, y_mat = matrices(frequency, ref_velocity)
    rows = zone_index.shape[1]
    both = lax.all_gather(
        jnp.concatenate([zone_index, blend_weight], axis=1), "depth", axis=0, tiled=True
    )
    pieces = migrate(
        lat_size, source_field, receiver_field, both[:, :rows], both[:, rows:], x_mat, y_mat
    )
    blocks = pieces.reshape(groups, -1, *pieces.shape[1:])
    arrived = lax.all_to_all(blocks, "depth", split_axis=0, concat_axis=0, tiled=True)
    return arrived.sum(axis=0) / freq_count


def solution(mesh):
    in_specs = (
        P(None, None, "lat", None),
        P(None, None, "lat", None),
        P("depth", "lat", None),
        P("depth", "lat", None),
        P(),
        P(),
    )
    out_specs = P("depth", "lat", None)
    return jax.shard_map(
        functools.partial(local, mesh.shape["lat"]),
        mesh=mesh, in_specs=in_specs, out_specs=out_specs, check_vma=False,
    )
```

time: 729 us -> 213 us (0.29)
  other arithmetic: 389 us -> 6.94 us
  Pallas kernels: 0 us -> 106 us
  starting transfers between devices: 89.8 us -> 0.01 us
  local copies, waits for them, and re-layouts: 83.8 us -> 5.39 us
  waiting for transfers between devices: 101 us -> 33.6 us
    reduce_sum x18 -> x2, other arithmetic: 256 us -> 0.31 us  [the longest x1 0.19 us: local(): return arrived.sum(axis=0) / freq_count]
    pallas_call x0 -> x1, Pallas kernels: none -> 106 us  [migrate(): pl.pallas_call(functools.partial(body, lat_size), out_shape=jax.ShapeDtyp...]
    ppermute x32 -> x0, starting transfers between devices: 89.8 us -> none  [the longest x16 58.6 us: padded_2(): lax.ppermute(lax.slice_in_dim(block, 0, width, axis=dim), axis, backward)]
    ppermute x32 -> x0, waiting for transfers between devices: 64.5 us -> none  [the longest x16 64.5 us: padded_2(): lax.ppermute(lax.slice_in_dim(block, block.shape[dim] - width, None, axis...]
    add x32 -> x1, other arithmetic: 48.6 us -> 0.11 us  [matrices(): d_im = c_re * turn_sin[:, None] + c_im * turn_cos[:, None]]
    sub x32 -> x2, other arithmetic: 48.5 us -> 0.01 us  [the longest x1 0.01 us: matrices(): distance = jnp.abs(k - HALF - n)]
    mul x80 -> x0, local copies, waits for them, and re-layouts: 39.5 us -> none  [convolve_rows(): out_re = out_re + coef_re * part_re - coef_im * part_im]
    slice x50 -> x1, local copies, waits for them, and re-layouts: 34.7 us -> 4.77 us  [local(): both[:, rows:]]
  transfers between devices with their start and end apart: 33 -> 1, of which waited for: 17 -> 1; matrix products, arithmetic and copies ran while one was open for 9% -> 2% of each run, Pallas kernels for 0% -> 0%
where the time goes in v1:
time: 213 us; the launch traced here: 210 us
  Pallas kernels  106 us (50%)
  blocking collectives  44 us (21%)
  waiting for transfers between devices  33.6 us (16%)
  between operations  14.2 us (7%)
  other arithmetic  6.94 us (3%)
  local copies, waits for them, and re-layouts  5.39 us (3%)
    pallas_call x1, Pallas kernels, migrate(): pl.pallas_call(functools.partial(body, lat_size), out_shape=jax.ShapeDtyp...  106 us
    all_to_all x1, blocking collectives, local(): lax.all_to_all(blocks, 'depth', split_axis=0, concat_axis=0, tiled=True)  44 us
    all_gather x1, waiting for transfers between devices, local(): lax.all_gather(jnp.concatenate([zone_index, blend_weight], axis=1), 'dept...  33.6 us
    slice x1, local copies, waits for them, and re-layouts, local(): both[:, rows:]  4.77 us
  transfers between devices with their start and end apart: 1, of which 1 were waited for; matrix products, arithmetic and copies ran while one was open for 2% of the time, Pallas kernels for 0%

profile of v1, /device:TPU:97, one launch (start us, length us, event | category | flops | bytes accessed | tf_op | source)
XLA Modules:
  0.0 210.3 jit_solution(2660910019076273281)
XLA Ops:
  6.5 0.0 copy-start.1
  6.5 0.0 all-gather.2.cloned.1.call-start
  6.5 2.3 %pad_add_fusion = s32[4,64,1024]{2,1,0:T(8,128)} fusion(s32[4,32,1024]{2,1,0:T(8,128)} %param.9, s32[4,32,1024]{2,1,0:T(8,128)} %param.8), kind=kLoop, calls=%fused_computation.4 | loop fusion | flops 262144 | bytes 2097152 | tf_op jit(solution)/shard_map/concatenate | solution.py:272
  8.8 0.0 all-gather.2.cloned.1.call-update
  8.9 0.0 copy-done.1
  8.9 0.6 dynamic_slice.4
  10.2 0.0 copy-done
  10.3 0.1 fusion.29
  10.4 0.1 multiply_add_fusion
  10.6 0.1 select_select_fusion.3
  10.7 0.1 fusion.36
  10.8 0.1 maximum_maximum_fusion.1
  10.9 0.7 pad_maximum_fusion.1.x_mat
  11.7 0.2 fusion.10
  11.9 0.3 select_select_fusion.1
  12.2 0.3 select_select_fusion
  12.5 0.1 reduce-precision_convert_fusion
  12.6 1.3 pad_maximum_fusion.y_mat
  13.9 33.6 %all-gather.2.cloned.1.call-done = s32[16,64,1024]{2,1,0:T(8,128)} async-done(((s32[4,64,1024]{2,1,0:T(8,128)}), s32[16,64,1024]{2,1,0:T(8,128)}) %all-gather.2.cloned.1.call-update) | async-done | bytes 4194320 | tf_op jit(solution)/shard_map/all_gather | solution.py:271
  47.5 4.8 %fusion.38 = (s32[16,32,1024]{2,1,0:T(8,128)}, s32[16,32,1024]{2,1,0:T(8,128)}) fusion(s32[16,64,1024]{2,1,0:T(8,128)} %all-gather.2.cloned.1.call-done), kind=kLoop, calls=%fused_computation.101 | loop fusion | bytes 8388608 | tf_op jit(solution)/shard_map/slice | solution.py:275
  52.3 106.2 %shard_map.64 = f32[16,32,1024]{2,1,0:T(8,128)} custom-call(f32[2,4,32,1024]{3,2,1,0:T(8,128)} %source.1, f32[2,4,32,1024]{3,2,1,0:T(8,128)} %receiver.1, s32[16,32,1024]{2,1,0:T(8,128)} %get-tuple-element.10.zone, s32[16,32,1024]{2,1,0:T(8,128)} %get-tuple-element.9.blend, bf16[128,192]{1,0:T(8,128)(2,1)} %pad_maximum_fusion.1.x_mat, ...), custom_call_target="tpu_custom_call" | custom-call | tf_op jit(solution)/shard_map/pallas_call | solution.py:244
  158.4 44.0 %all_to_all.5 = f32[4,4,32,1024]{3,2,1,0:T(8,128)S(1)} all-to-all(f32[4,4,32,1024]{3,2,1,0:T(8,128)} %bitcast.69), channel_id=1, replica_groups=mesh['depth'=4,'lat'=32] {'depth'}, dimensions={0} | all-to-all | bytes 4194304 | tf_op jit(solution)/shard_map/all_to_all | solution.py:278
  202.4 0.2 reduce_sum.29
  202.6 0.8 broadcast_multiply_fusion
  (15 shorter events, 0.2 us)
Async XLA Ops:
  6.5 2.3 %copy-start.1 = (s32[4]{0:T(128)S(1)}, s32[4]{0:T(128)}, u32[]{:S(2)}) copy-start(s32[4]{0:T(128)} %param.11) | copy-start | bytes 52
  6.5 3.6 %copy-start = (f32[4]{0:T(128)S(1)}, f32[4]{0:T(128)}, u32[]{:S(2)}) copy-start(f32[4]{0:T(128)} %param.10) | copy-start | bytes 52
  6.5 41.0 %all-gather.2.cloned.1.call-start = ((), (), s32[]{:S(2)}) async-start(), calls=%async_computation.1 | async-start | bytes 5242880 | tf_op jit(solution)/shard_map/all_gather | solution.py:271
Sparse Core Ops, SparseCore 0:
  9.0 38.4 all-gather.1

commit v2 on v1

v2 whole, which is shorter than its diff:
```python
import functools
import math

import jax
import jax.numpy as jnp
from jax import lax
from jax.experimental import pallas as pl
from jax.experimental.pallas import tpu as pltpu
from jax.sharding import PartitionSpec as P

HALF = 7
BLEND = 16
LANES = 128
PAD = 128
STEP = LANES - 2 * HALF
HALO = 8
GROUP = 16

cell_width = 5.0
depth_step = 10.0
taper_width = 16.0


def kernels(frequency, ref_velocity):
    offsets = jnp.arange(0, HALF + 1, dtype=jnp.int32).astype(jnp.float32)
    wavenumber = 2.0 * math.pi * frequency.astype(jnp.float32) / ref_velocity
    curvature = wavenumber * (cell_width * cell_width / (2.0 * depth_step))
    phase_turn = wavenumber * depth_step
    chirp_angle = curvature[:, None] * (offsets * offsets)[None, :]
    envelope = jnp.exp(-offsets * offsets / taper_width)
    raw_re = envelope * jnp.cos(chirp_angle)
    raw_im = envelope * jnp.sin(chirp_angle)
    both = jnp.where(offsets == 0.0, 1.0, 2.0)
    magnitude = jnp.sqrt(
        jnp.sum(both * raw_re, axis=-1) ** 2 + jnp.sum(both * raw_im, axis=-1) ** 2
    )[:, None]
    return raw_re / magnitude, raw_im / magnitude, jnp.cos(phase_turn), jnp.sin(phase_turn)


def split(x):
    high = lax.reduce_precision(x, 8, 7)
    return high.astype(jnp.bfloat16), (x - high).astype(jnp.bfloat16)


def banded(taps, distance, keep):
    out = jnp.zeros((taps.shape[0],) + distance.shape, jnp.float32)
    for m in range(HALF + 1):
        out = jnp.where((distance == m) & keep, taps[:, m][:, None, None], out)
    return out


def matrices(frequency, ref_velocity):
    c_re, c_im, turn_cos, turn_sin = kernels(frequency, ref_velocity)
    refs = c_re.shape[0]
    r = jnp.arange(GROUP)[:, None]
    k = jnp.arange(2 * GROUP)[None, :]
    distance = jnp.abs(k - HALO - r)
    a_re, a_im = (banded(t, distance, True) for t in (c_re, c_im))
    x_mat = jnp.concatenate(
        [jnp.concatenate([a_re, -a_im], 2), jnp.concatenate([a_im, a_re], 2)], 1
    ).reshape(refs * 2 * GROUP, 4 * GROUP)
    x_high, x_low = split(x_mat)
    x_all = jnp.concatenate([x_high, x_high, x_low], 1)
    d_re = c_re * turn_cos[:, None] - c_im * turn_sin[:, None]
    d_im = c_re * turn_sin[:, None] + c_im * turn_cos[:, None]
    k = jnp.arange(LANES)[:, None]
    n = jnp.arange(LANES)[None, :]
    distance = jnp.abs(k - HALF - n)
    b_re, b_im = (banded(t, distance, n < STEP) for t in (d_re, d_im))
    y_mat = jnp.concatenate(
        [jnp.concatenate([b_re, b_im], 2), jnp.concatenate([-b_im, b_re], 2)], 1
    )
    y_high, y_low = split(y_mat)
    return x_all, jnp.concatenate([y_high, y_high, y_low], 1)


def two_parts(x):
    high = x.astype(jnp.bfloat16)
    return high, (x - high.astype(jnp.float32)).astype(jnp.bfloat16)


def body(
    lat_size, source, receiver, zone, blend, x_mat, y_mat,
    image, field, halo, table, weights, xbuf, ybuf, part, arrived,
    load_sem, table_sem, table_sent, send_sem, recv_sem, part_sem, part_sent,
):
    own_levels, rows, cols = zone.shape
    levels, width_all = table.shape[1], table.shape[3]
    depths = levels // own_levels
    pairs = x_mat.shape[0]
    refs = y_mat.shape[1]
    half = part.shape[2]
    windows = -(-width_all // STEP)
    lat = lax.axis_index("lat")
    me = lax.axis_index("depth")
    side, core = me // 2, lax.rem(me, 2)
    has_up = lat > 0
    has_down = lat < lat_size - 1
    inner = pl.ds(PAD, width_all)

    def columns_of(device):
        return pl.ds(pl.multiple_of((device // 2) * (cols - width_all), LANES), width_all)

    peers = [side * 2 + 1 - core, (1 - side) * 2 + core, (1 - side) * 2 + 1 - core]
    tables = (zone, blend)

    loads = [
        pltpu.make_async_copy(
            ref.at[:, core * pairs + q, :, columns_of(me)],
            field.at[2 * q + f, :, :, inner],
            load_sem.at[2 * q + f],
        )
        for q in range(pairs)
        for f, ref in enumerate((source, receiver))
    ]
    for load in loads:
        load.start()

    def own_table(a, n):
        at = me * own_levels + n
        return pltpu.make_async_copy(
            tables[a].at[n, :, columns_of(me)], table.at[a, at], table_sem.at[a, at]
        )

    def peer_table(i, a, n):
        at = me * own_levels + n
        return pltpu.make_async_remote_copy(
            src_ref=tables[a].at[n, :, columns_of(peers[i])],
            dst_ref=table.at[a, at],
            send_sem=table_sent.at[i, a, n],
            recv_sem=table_sem.at[a, at],
            device_id={"depth": peers[i]},
        )

    every_table = [(i, a, n) for n in range(own_levels) for i in range(3) for a in range(2)]
    for n in range(own_levels):
        for a in range(2):
            own_table(a, n).start()
    halo[...] = jnp.zeros_like(halo)
    for s in range(2 * pairs):
        for c in range(2):
            field[s, c, :, 0:PAD] = jnp.zeros((rows, PAD), jnp.float32)
            field[s, c, :, PAD + width_all :] = jnp.zeros((rows, PAD), jnp.float32)

    barrier = pltpu.get_barrier_semaphore()

    @pl.when(has_up)
    def _():
        pl.semaphore_signal(barrier, inc=1, device_id={"lat": lat - 1})

    @pl.when(has_down)
    def _():
        pl.semaphore_signal(barrier, inc=1, device_id={"lat": lat + 1})

    for peer in peers:
        pl.semaphore_signal(barrier, inc=1, device_id={"depth": peer})
    pl.semaphore_wait(
        barrier, len(peers) + has_up.astype(jnp.int32) + has_down.astype(jnp.int32)
    )

    def to_up(s, slot):
        return pltpu.make_async_remote_copy(
            src_ref=field.at[s, :, pl.ds(0, HALO), inner],
            dst_ref=halo.at[slot, s, 1, :, :, inner],
            send_sem=send_sem.at[s, 0],
            recv_sem=recv_sem.at[slot, s, 1],
            device_id={"lat": lat - 1},
        )

    def to_down(s, slot):
        return pltpu.make_async_remote_copy(
            src_ref=field.at[s, :, pl.ds(rows - HALO, HALO), inner],
            dst_ref=halo.at[slot, s, 0, :, :, inner],
            send_sem=send_sem.at[s, 1],
            recv_sem=recv_sem.at[slot, s, 0],
            device_id={"lat": lat + 1},
        )

    def each_side(act_up, act_down):
        @pl.when(has_up)
        def _():
            act_up()

        @pl.when(has_down)
        def _():
            act_down()

    def send(s, slot):
        each_side(lambda: to_up(s, slot).start(), lambda: to_down(s, slot).start())

    def wait_sent(s, slot):
        each_side(lambda: to_up(s, slot).wait_send(), lambda: to_down(s, slot).wait_send())

    def wait_arrived(s, slot):
        each_side(lambda: to_down(s, slot).wait_recv(), lambda: to_up(s, slot).wait_recv())

    for s in range(2 * pairs):
        loads[s].wait()
        if s % 2 == 1:
            field[s, 1] = -field[s, 1]
        send(s, 0)
    for one in every_table:
        peer_table(*one).start()

    def part_copy(z):
        return pltpu.make_async_remote_copy(
            src_ref=part.at[z],
            dst_ref=arrived.at[lax.rem(z, own_levels), me],
            send_sem=part_sent.at[z],
            recv_sem=part_sem.at[lax.rem(z, own_levels), me],
            device_id={"depth": z // own_levels},
        )

    def level(z, carry):
        slot = lax.rem(z, 2)
        for a in range(2):
            pltpu.make_async_copy(table.at[a, z], table.at[a, z], table_sem.at[a, z]).wait()
        for w in range(windows):
            width = min(STEP, width_all - w * STEP)
            here = pl.ds(w * STEP, width)
            which = table[0, z, :, here]
            upper = table[1, z, :, here].astype(jnp.float32) * (1.0 / BLEND)
            lower = 1.0 - upper
            for j in range(refs):
                weights[j, w * rows : (w + 1) * rows, 0:width] = jnp.where(
                    which == j, lower, jnp.where(which == j - 1, upper, 0.0)
                )
        for s in range(2 * pairs):
            q = s // 2
            wait_arrived(s, slot)
            for w in range(windows):
                at = pl.ds(PAD + w * STEP - HALF, LANES)
                parts = []
                for group in range(rows // GROUP):
                    column = []
                    for c in range(2):
                        first = group * GROUP - HALO
                        pieces = []
                        if first < 0:
                            pieces.append(halo[slot, s, 0, c, :, at])
                        low, high = max(first, 0), min(first + 2 * GROUP, rows)
                        pieces.append(field[s, c, low:high, at])
                        if first + 2 * GROUP > rows:
                            pieces.append(halo[slot, s, 1, c, :, at])
                        column.append(jnp.concatenate(pieces, 0))
                    parts.append(jnp.concatenate(column, 0))
                high, low = two_parts(jnp.concatenate(parts, 1))
                out = jnp.dot(
                    x_mat[q],
                    jnp.concatenate([high, low, high], 0),
                    preferred_element_type=jnp.float32,
                )
                for p, values in enumerate(two_parts(out)):
                    for j in range(refs):
                        for c in range(2):
                            for group in range(rows // GROUP):
                                top = (j * 2 + c) * GROUP
                                left = group * LANES
                                xbuf[
                                    j,
                                    w * rows + group * GROUP : w * rows + (group + 1) * GROUP,
                                    (p * 2 + c) * LANES : (p * 2 + c + 1) * LANES,
                                ] = values[top : top + GROUP, left : left + LANES]
            wait_sent(s, slot)
            for j in range(refs):
                ybuf[j] = jnp.dot(
                    jnp.concatenate([xbuf[j], xbuf[j, :, 0 : 2 * LANES]], 1),
                    y_mat[q, j],
                    preferred_element_type=jnp.float32,
                )
            for w in range(windows):
                width = min(STEP, width_all - w * STEP)
                block = slice(w * rows, (w + 1) * rows)
                for c in range(2):
                    total = weights[0, block, 0:width] * ybuf[0, block, c * LANES : c * LANES + width]
                    for j in range(1, refs):
                        total = total + (
                            weights[j, block, 0:width]
                            * ybuf[j, block, c * LANES : c * LANES + width]
                        )
                    field[s, c, :, pl.ds(PAD + w * STEP, width)] = total

            @pl.when(z < levels - 1)
            def _():
                send(s, 1 - slot)

        mine = pl.ds(pl.multiple_of(PAD + side * (width_all - half), LANES), half)
        total = jnp.zeros((rows, half), jnp.float32)
        for q in range(pairs):
            total = total + field[2 * q, 0, :, mine] * field[2 * q + 1, 0, :, mine]
            total = total - field[2 * q, 1, :, mine] * field[2 * q + 1, 1, :, mine]

        @pl.when(z // own_levels == me)
        def _():
            arrived[lax.rem(z, own_levels), me] = total

        @pl.when(z // own_levels != me)
        def _():
            part[z] = total
            part_copy(z).start()

        return carry

    lax.fori_loop(0, levels, level, 0)

    for one in every_table:
        peer_table(*one).wait_send()

    def sent(z, carry):
        @pl.when(z // own_levels != me)
        def _():
            part_copy(z).wait_send()

        return carry

    lax.fori_loop(0, levels, sent, 0)
    for n in range(own_levels):
        for d in range(depths):
            @pl.when(d != me)
            def _():
                pltpu.make_async_copy(
                    arrived.at[n, d], arrived.at[n, d], part_sem.at[n, d]
                ).wait()

        for h in range(depths // 2):
            image[n, :, h * half : (h + 1) * half] = (
                arrived[n, 2 * h] + arrived[n, 2 * h + 1]
            ) * (1.0 / (2 * pairs))


def migrate(lat_size, depths, source, receiver, zone, blend, x_mat, y_mat):
    own_levels, rows, cols = zone.shape
    levels = depths * own_levels
    pairs, refs = y_mat.shape[:2]
    streams = 2 * pairs
    half = cols // 2
    width = half + -(-HALF * levels // LANES) * LANES
    windows = -(-width // STEP)
    vmem = pl.BlockSpec(memory_space=pltpu.VMEM)
    hbm = pl.BlockSpec(memory_space=pl.ANY)
    wide = width + 2 * PAD
    dma = pltpu.SemaphoreType.DMA
    return pl.pallas_call(
        functools.partial(body, lat_size),
        out_shape=jax.ShapeDtypeStruct((own_levels, rows, cols), jnp.float32),
        in_specs=[hbm, hbm, hbm, hbm, vmem, vmem],
        out_specs=vmem,
        scratch_shapes=[
            pltpu.VMEM((streams, 2, rows, wide), jnp.float32),
            pltpu.VMEM((2, streams, 2, 2, HALO, wide), jnp.float32),
            pltpu.VMEM((2, levels, rows, width), jnp.int32),
            pltpu.VMEM((refs, windows * rows, LANES), jnp.float32),
            pltpu.VMEM((refs, windows * rows, 4 * LANES), jnp.bfloat16),
            pltpu.VMEM((refs, windows * rows, 2 * LANES), jnp.float32),
            pltpu.VMEM((levels, rows, half), jnp.float32),
            pltpu.VMEM((own_levels, depths, rows, half), jnp.float32),
            dma((streams,)),
            dma((2, levels)),
            dma((3, 2, own_levels)),
            dma((streams, 2)),
            dma((2, streams, 2)),
            dma((own_levels, depths)),
            dma((levels,)),
        ],
        compiler_params=pltpu.CompilerParams(
            collective_id=0, has_side_effects=True, vmem_limit_bytes=60 * 2**20
        ),
    )(source, receiver, zone, blend, x_mat, y_mat)


def local(lat_size, source_field, receiver_field, zone_index, blend_weight, ref_velocity, frequencies):
    depths = lax.axis_size("depth")
    pairs = source_field.shape[1] // 2
    core = lax.rem(lax.axis_index("depth"), 2)
    chosen = lax.dynamic_slice_in_dim(frequencies, core * pairs, pairs)
    made = [matrices(chosen[q], ref_velocity) for q in range(pairs)]
    x_mat, y_mat = (jnp.stack(m) for m in zip(*made))
    return migrate(
        lat_size, depths, source_field, receiver_field, zone_index, blend_weight, x_mat, y_mat
    )


def solution(mesh):
    in_specs = (
        P(None, None, "lat", None),
        P(None, None, "lat", None),
        P("depth", "lat", None),
        P("depth", "lat", None),
        P(),
        P(),
    )
    out_specs = P("depth", "lat", None)
    return jax.shard_map(
        functools.partial(local, mesh.shape["lat"]),
        mesh=mesh, in_specs=in_specs, out_specs=out_specs, check_vma=False,
    )
```

time: 213 us -> 148 us (0.69)
  the two profiles are of different devices: /device:TPU:97 before, /device:TPU:103 now
where the time goes in v2:
time: 148 us
  Pallas kernels  137 us (93%)
  other arithmetic  6.34 us (4%)
  local copies, waits for them, and re-layouts  3.26 us (2%)
  between operations  1.55 us (1%)
    pallas_call x1, Pallas kernels, migrate(): pl.pallas_call(functools.partial(body, lat_size), out_shape=jax.ShapeDtyp...  137 us
    another operation x6, other arithmetic, local(): x_mat, y_mat = (jnp.stack(m) for m in zip(*made))  2.97 us

profile of v2, /device:TPU:103, one launch (start us, length us, event | category | flops | bytes accessed | tf_op | source)
XLA Modules:
  0.0 148.3 jit_solution(441057414233444301)
XLA Ops:
  0.0 0.7 dynamic_slice.3
  0.7 0.6 fusion.50
  2.6 0.7 multiply_cosine_fusion.2
  3.4 0.1 fusion.31
  3.6 0.1 multiply_add_fusion.1
  3.7 0.2 fusion.12
  3.9 0.3 select_select_fusion.2
  4.2 0.3 select_select_fusion.3
  4.6 0.1 reduce-precision_convert_fusion.1
  4.7 0.1 maximum_bitcast_fusion
  4.8 0.3 select_select_fusion
  5.2 0.3 select_select_fusion.1
  5.5 0.2 reduce-precision_convert_fusion
  5.6 0.1 maximum_bitcast_fusion.1
  5.7 1.9 %pad_maximum_fusion.y_mat = bf16[2,4,768,256]{3,2,1,0:T(8,128)(2,1)} fusion(bf16[1,4,768,256]{3,2,1,0:T(8,128)(2,1)S(1)} %maximum_bitcast_fusion.1, bf16[1,4,768,256]{3,2,1,0:T(8,128)(2,1)S(1)} %maximum_bitcast_fusion), kind=kLoop, calls=%fused_computation | loop fusion | flops 1572864 | bytes 6291456 | tf_op jit(solution)/shard_map/stack | solution.py:377
  7.7 0.1 fusion.46
  7.8 0.1 select_select_fusion.7
  8.0 0.1 maximum_bitcast_fusion.2
  8.1 0.1 fusion.47
  8.3 0.1 select_select_fusion.5
  8.5 0.1 maximum_bitcast_fusion.3
  8.6 0.7 pad_maximum_fusion.1.x_mat
  9.3 137.1 %shard_map.64 = f32[4,32,1024]{2,1,0:T(8,128)} custom-call(f32[2,4,32,1024]{3,2,1,0:T(8,128)} %source.1, f32[2,4,32,1024]{3,2,1,0:T(8,128)} %receiver.1, s32[4,32,1024]{2,1,0:T(8,128)} %zone.1, s32[4,32,1024]{2,1,0:T(8,128)} %blend.1, bf16[2,128,192]{2,1,0:T(8,128)(2,1)} %pad_maximum_fusion.1.x_mat, bf16[2,4,768,256]{3,2,1,0:T(8,128)(2,1)} %pad_maximum_fusion.y_mat), custom_call_target="tpu_custom_call" | custom-call | tf_op jit(solution)/shard_map/pallas_call | solution.py:343
  146.4 1.9 %copy.8 = f32[4,32,1024]{2,1,0:T(8,128)} copy(f32[4,32,1024]{2,1,0:T(8,128)} %shard_map.64) | data formatting | bytes 1048576
  (21 shorter events, 0.4 us)

commit v3 on v2

--- a/solution.py
+++ b/solution.py
@@ -15,6 +15,7 @@
 STEP = LANES - 2 * HALF
 HALO = 8
 GROUP = 16
+AHEAD = 2
 
 cell_width = 5.0
 depth_step = 10.0
@@ -82,7 +83,7 @@
 def body(
     lat_size, source, receiver, zone, blend, x_mat, y_mat,
     image, field, halo, table, weights, xbuf, ybuf, part, arrived,
-    load_sem, table_sem, table_sent, send_sem, recv_sem, part_sem, part_sent,
+    load_sem, table_sem, table_sent, passed_sent, send_sem, recv_sem, part_sem, part_sent,
 ):
     own_levels, rows, cols = zone.shape
     levels, width_all = table.shape[1], table.shape[3]
@@ -122,17 +123,36 @@
             tables[a].at[n, :, columns_of(me)], table.at[a, at], table_sem.at[a, at]
         )
 
-    def peer_table(i, a, n):
+    partner = peers[0]
+    far_levels = 2 * own_levels
+
+    def peer_table(across, a, n):
         at = me * own_levels + n
+        peer = (1 - side) * 2 + a if across else partner
         return pltpu.make_async_remote_copy(
-            src_ref=tables[a].at[n, :, columns_of(peers[i])],
+            src_ref=tables[a].at[n, :, columns_of(peer)],
             dst_ref=table.at[a, at],
-            send_sem=table_sent.at[i, a, n],
+            send_sem=table_sent.at[int(across), a, n],
             recv_sem=table_sem.at[a, at],
-            device_id={"depth": peers[i]},
-        )
-
-    every_table = [(i, a, n) for n in range(own_levels) for i in range(3) for a in range(2)]
+            device_id={"depth": peer},
+        )
+
+    def passed(i):
+        at = (1 - side) * far_levels + i
+        return pltpu.make_async_remote_copy(
+            src_ref=table.at[core, at],
+            dst_ref=table.at[core, at],
+            send_sem=passed_sent.at[i],
+            recv_sem=table_sem.at[core, at],
+            device_id={"depth": partner},
+        )
+
+    def pass_on(i):
+        at = (1 - side) * far_levels + i
+        there = table.at[core, at]
+        pltpu.make_async_copy(there, there, table_sem.at[core, at]).wait()
+        passed(i).start()
+
     for n in range(own_levels):
         for a in range(2):
             own_table(a, n).start()
@@ -199,8 +219,16 @@
         if s % 2 == 1:
             field[s, 1] = -field[s, 1]
         send(s, 0)
-    for one in every_table:
-        peer_table(*one).start()
+    for n in range(own_levels):
+        @pl.when(core == 0)
+        def _():
+            for a in range(2):
+                peer_table(True, a, n).start()
+
+        for a in range(2):
+            peer_table(False, a, n).start()
+    for i in range(AHEAD):
+        pass_on(i)
 
     def part_copy(z):
         return pltpu.make_async_remote_copy(
@@ -213,8 +241,23 @@
 
     def level(z, carry):
         slot = lax.rem(z, 2)
+
+        @pl.when(jnp.logical_and(core == 1, z < own_levels))
+        def _():
+            for a in range(2):
+                peer_table(True, a, z).start()
+
+        @pl.when(z + AHEAD < far_levels)
+        def _():
+            pass_on(z + AHEAD)
+
         for a in range(2):
-            pltpu.make_async_copy(table.at[a, z], table.at[a, z], table_sem.at[a, z]).wait()
+            taken = jnp.logical_and(z // far_levels != side, core == a)
+
+            @pl.when(jnp.logical_not(taken))
+            def _():
+                pltpu.make_async_copy(table.at[a, z], table.at[a, z], table_sem.at[a, z]).wait()
+
         for w in range(windows):
             width = min(STEP, width_all - w * STEP)
             here = pl.ds(w * STEP, width)
@@ -303,8 +346,12 @@
 
     lax.fori_loop(0, levels, level, 0)
 
-    for one in every_table:
-        peer_table(*one).wait_send()
+    for n in range(own_levels):
+        for a in range(2):
+            peer_table(False, a, n).wait_send()
+            peer_table(True, a, n).wait_send()
+    for i in range(far_levels):
+        passed(i).wait_send()
 
     def sent(z, carry):
         @pl.when(z // own_levels != me)
@@ -356,7 +403,8 @@
             pltpu.VMEM((own_levels, depths, rows, half), jnp.float32),
             dma((streams,)),
             dma((2, levels)),
-            dma((3, 2, own_levels)),
+            dma((2, 2, own_levels)),
+            dma((2 * own_levels,)),
             dma((streams, 2)),
             dma((2, streams, 2)),
             dma((own_levels, depths)),

time: 148 us -> 130 us (0.88)
  the two profiles are of different devices: /device:TPU:103 before, /device:TPU:97 now
where the time goes in v3:
time: 130 us; the launch traced here: 129 us
  Pallas kernels  118 us (91%)
  other arithmetic  6.34 us (5%)
  local copies, waits for them, and re-layouts  3.26 us (3%)
  between operations  1.55 us (1%)
    pallas_call x1, Pallas kernels, migrate(): pl.pallas_call(functools.partial(body, lat_size), out_shape=jax.ShapeDtyp...  118 us
    another operation x6, other arithmetic, local(): x_mat, y_mat = (jnp.stack(m) for m in zip(*made))  2.97 us

profile of v3, /device:TPU:97, one launch (start us, length us, event | category | flops | bytes accessed | tf_op | source)
XLA Modules:
  0.0 129.5 jit_solution(9853069525055985275)
XLA Ops:
  0.0 0.7 dynamic_slice.3
  0.7 0.6 fusion.50
  2.6 0.7 multiply_cosine_fusion.2
  3.4 0.1 fusion.31
  3.6 0.1 multiply_add_fusion.1
  3.7 0.2 fusion.12
  3.9 0.3 select_select_fusion.2
  4.2 0.3 select_select_fusion.3
  4.6 0.1 reduce-precision_convert_fusion.1
  4.7 0.1 maximum_bitcast_fusion
  4.8 0.3 select_select_fusion
  5.2 0.3 select_select_fusion.1
  5.5 0.2 reduce-precision_convert_fusion
  5.6 0.1 maximum_bitcast_fusion.1
  5.7 1.9 %pad_maximum_fusion.y_mat = bf16[2,4,768,256]{3,2,1,0:T(8,128)(2,1)} fusion(bf16[1,4,768,256]{3,2,1,0:T(8,128)(2,1)S(1)} %maximum_bitcast_fusion.1, bf16[1,4,768,256]{3,2,1,0:T(8,128)(2,1)S(1)} %maximum_bitcast_fusion), kind=kLoop, calls=%fused_computation | loop fusion | flops 1572864 | bytes 6291456 | tf_op jit(solution)/shard_map/stack | solution.py:425
  7.7 0.1 fusion.46
  7.8 0.1 select_select_fusion.7
  8.0 0.1 maximum_bitcast_fusion.2
  8.1 0.1 fusion.47
  8.3 0.1 select_select_fusion.5
  8.5 0.1 maximum_bitcast_fusion.3
  8.6 0.7 pad_maximum_fusion.1.x_mat
  9.3 118.3 %shard_map.64 = f32[4,32,1024]{2,1,0:T(8,128)} custom-call(f32[2,4,32,1024]{3,2,1,0:T(8,128)} %source.1, f32[2,4,32,1024]{3,2,1,0:T(8,128)} %receiver.1, s32[4,32,1024]{2,1,0:T(8,128)} %zone.1, s32[4,32,1024]{2,1,0:T(8,128)} %blend.1, bf16[2,128,192]{2,1,0:T(8,128)(2,1)} %pad_maximum_fusion.1.x_mat, bf16[2,4,768,256]{3,2,1,0:T(8,128)(2,1)} %pad_maximum_fusion.y_mat), custom_call_target="tpu_custom_call" | custom-call | tf_op jit(solution)/shard_map/pallas_call | solution.py:390
  127.6 1.9 %copy.8 = f32[4,32,1024]{2,1,0:T(8,128)} copy(f32[4,32,1024]{2,1,0:T(8,128)} %shard_map.64) | data formatting | bytes 1048576
  (21 shorter events, 0.4 us)

commit v4 on v3

--- a/solution.py
+++ b/solution.py
@@ -15,6 +15,7 @@
 STEP = LANES - 2 * HALF
 HALO = 8
 GROUP = 16
+FAR = 16
 AHEAD = 2
 
 cell_width = 5.0
@@ -82,8 +83,9 @@
 
 def body(
     lat_size, source, receiver, zone, blend, x_mat, y_mat,
-    image, field, halo, table, weights, xbuf, ybuf, part, arrived,
-    load_sem, table_sem, table_sent, passed_sent, send_sem, recv_sem, part_sem, part_sent,
+    image, field, middle, halo, table, rim, weights, xbuf, ybuf, part, inbox, arrived,
+    load_sem, table_sem, table_sent, passed_sent, rim_sem, rim_sent,
+    send_sem, recv_sem, part_sem, part_sent, inbox_sem,
 ):
     own_levels, rows, cols = zone.shape
     levels, width_all = table.shape[1], table.shape[3]
@@ -157,10 +159,13 @@
         for a in range(2):
             own_table(a, n).start()
     halo[...] = jnp.zeros_like(halo)
-    for s in range(2 * pairs):
-        for c in range(2):
-            field[s, c, :, 0:PAD] = jnp.zeros((rows, PAD), jnp.float32)
-            field[s, c, :, PAD + width_all :] = jnp.zeros((rows, PAD), jnp.float32)
+    rim[...] = jnp.full(rim.shape, -2, jnp.int32)
+    for ref in (field, middle):
+        outside = jnp.zeros((ref.shape[2], PAD), jnp.float32)
+        for s in range(2 * pairs):
+            for c in range(2):
+                ref[s, c, :, 0:PAD] = outside
+                ref[s, c, :, PAD + width_all :] = outside
 
     barrier = pltpu.get_barrier_semaphore()
 
@@ -178,19 +183,19 @@
         barrier, len(peers) + has_up.astype(jnp.int32) + has_down.astype(jnp.int32)
     )
 
-    def to_up(s, slot):
-        return pltpu.make_async_remote_copy(
-            src_ref=field.at[s, :, pl.ds(0, HALO), inner],
-            dst_ref=halo.at[slot, s, 1, :, :, inner],
+    def to_up(s, slot, count):
+        return pltpu.make_async_remote_copy(
+            src_ref=field.at[s, :, pl.ds(0, count), inner],
+            dst_ref=halo.at[slot, s, 1, :, pl.ds(0, count), inner],
             send_sem=send_sem.at[s, 0],
             recv_sem=recv_sem.at[slot, s, 1],
             device_id={"lat": lat - 1},
         )
 
-    def to_down(s, slot):
-        return pltpu.make_async_remote_copy(
-            src_ref=field.at[s, :, pl.ds(rows - HALO, HALO), inner],
-            dst_ref=halo.at[slot, s, 0, :, :, inner],
+    def to_down(s, slot, count):
+        return pltpu.make_async_remote_copy(
+            src_ref=field.at[s, :, pl.ds(rows - count, count), inner],
+            dst_ref=halo.at[slot, s, 0, :, pl.ds(FAR - count, count), inner],
             send_sem=send_sem.at[s, 1],
             recv_sem=recv_sem.at[slot, s, 0],
             device_id={"lat": lat + 1},
@@ -205,20 +210,54 @@
         def _():
             act_down()
 
-    def send(s, slot):
-        each_side(lambda: to_up(s, slot).start(), lambda: to_down(s, slot).start())
-
-    def wait_sent(s, slot):
-        each_side(lambda: to_up(s, slot).wait_send(), lambda: to_down(s, slot).wait_send())
-
-    def wait_arrived(s, slot):
-        each_side(lambda: to_down(s, slot).wait_recv(), lambda: to_up(s, slot).wait_recv())
+    def send(s, slot, count):
+        each_side(
+            lambda: to_up(s, slot, count).start(), lambda: to_down(s, slot, count).start()
+        )
+
+    def wait_sent(s, slot, count):
+        each_side(
+            lambda: to_up(s, slot, count).wait_send(),
+            lambda: to_down(s, slot, count).wait_send(),
+        )
+
+    def wait_arrived(s, slot, count):
+        each_side(
+            lambda: to_down(s, slot, count).wait_recv(),
+            lambda: to_up(s, slot, count).wait_recv(),
+        )
+
+    def rim_up(h):
+        return pltpu.make_async_remote_copy(
+            src_ref=table.at[:, 2 * h, pl.ds(0, HALO)],
+            dst_ref=rim.at[h, 1],
+            send_sem=rim_sent.at[h, 0],
+            recv_sem=rim_sem.at[h, 1],
+            device_id={"lat": lat - 1},
+        )
+
+    def rim_down(h):
+        return pltpu.make_async_remote_copy(
+            src_ref=table.at[:, 2 * h, pl.ds(rows - HALO, HALO)],
+            dst_ref=rim.at[h, 0],
+            send_sem=rim_sent.at[h, 1],
+            recv_sem=rim_sem.at[h, 0],
+            device_id={"lat": lat + 1},
+        )
+
+    def need(z):
+        for a in range(2):
+            taken = jnp.logical_and(z // far_levels != side, core == a)
+
+            @pl.when(jnp.logical_not(taken))
+            def _():
+                pltpu.make_async_copy(table.at[a, z], table.at[a, z], table_sem.at[a, z]).wait()
 
     for s in range(2 * pairs):
         loads[s].wait()
         if s % 2 == 1:
             field[s, 1] = -field[s, 1]
-        send(s, 0)
+        send(s, 0, HALO)
     for n in range(own_levels):
         @pl.when(core == 0)
         def _():
@@ -239,99 +278,91 @@
             device_id={"depth": z // own_levels},
         )
 
-    def level(z, carry):
-        slot = lax.rem(z, 2)
-
-        @pl.when(jnp.logical_and(core == 1, z < own_levels))
-        def _():
-            for a in range(2):
-                peer_table(True, a, z).start()
-
-        @pl.when(z + AHEAD < far_levels)
-        def _():
-            pass_on(z + AHEAD)
-
-        for a in range(2):
-            taken = jnp.logical_and(z // far_levels != side, core == a)
-
-            @pl.when(jnp.logical_not(taken))
-            def _():
-                pltpu.make_async_copy(table.at[a, z], table.at[a, z], table_sem.at[a, z]).wait()
-
+    def set_weights(z, pieces):
+        count = rows + (2 * HALO if pieces else 0)
         for w in range(windows):
             width = min(STEP, width_all - w * STEP)
             here = pl.ds(w * STEP, width)
-            which = table[0, z, :, here]
-            upper = table[1, z, :, here].astype(jnp.float32) * (1.0 / BLEND)
+            both = []
+            for a in range(2):
+                value = table[a, z, :, here]
+                if pieces:
+                    value = jnp.concatenate(
+                        [rim[z // 2, 0, a, :, here], value, rim[z // 2, 1, a, :, here]], 0
+                    )
+                both.append(value)
+            which = both[0]
+            upper = both[1].astype(jnp.float32) * (1.0 / BLEND)
             lower = 1.0 - upper
             for j in range(refs):
-                weights[j, w * rows : (w + 1) * rows, 0:width] = jnp.where(
+                weights[int(pieces), j, w * count : (w + 1) * count, 0:width] = jnp.where(
                     which == j, lower, jnp.where(which == j - 1, upper, 0.0)
                 )
-        for s in range(2 * pairs):
-            q = s // 2
-            wait_arrived(s, slot)
-            for w in range(windows):
+
+    def advance(q, wide_step, read, before_write, target, s):
+        groups = 3 if wide_step else 2
+        count = groups * GROUP
+        units = [(w, g) for w in range(windows) for g in range(groups)]
+        for first in range(0, len(units), 2):
+            chosen = units[first : first + 2]
+            parts = []
+            for w, g in chosen:
                 at = pl.ds(PAD + w * STEP - HALF, LANES)
-                parts = []
-                for group in range(rows // GROUP):
-                    column = []
+                parts.append(jnp.concatenate([read(c, g, at) for c in range(2)], 0))
+            high, low = two_parts(jnp.concatenate(parts, 1))
+            out = jnp.dot(
+                x_mat[q],
+                jnp.concatenate([high, low, high], 0),
+                preferred_element_type=jnp.float32,
+            )
+            for p, values in enumerate(two_parts(out)):
+                for j in range(refs):
                     for c in range(2):
-                        first = group * GROUP - HALO
-                        pieces = []
-                        if first < 0:
-                            pieces.append(halo[slot, s, 0, c, :, at])
-                        low, high = max(first, 0), min(first + 2 * GROUP, rows)
-                        pieces.append(field[s, c, low:high, at])
-                        if first + 2 * GROUP > rows:
-                            pieces.append(halo[slot, s, 1, c, :, at])
-                        column.append(jnp.concatenate(pieces, 0))
-                    parts.append(jnp.concatenate(column, 0))
-                high, low = two_parts(jnp.concatenate(parts, 1))
-                out = jnp.dot(
-                    x_mat[q],
-                    jnp.concatenate([high, low, high], 0),
-                    preferred_element_type=jnp.float32,
-                )
-                for p, values in enumerate(two_parts(out)):
-                    for j in range(refs):
-                        for c in range(2):
-                            for group in range(rows // GROUP):
-                                top = (j * 2 + c) * GROUP
-                                left = group * LANES
-                                xbuf[
-                                    j,
-                                    w * rows + group * GROUP : w * rows + (group + 1) * GROUP,
-                                    (p * 2 + c) * LANES : (p * 2 + c + 1) * LANES,
-                                ] = values[top : top + GROUP, left : left + LANES]
-            wait_sent(s, slot)
-            for j in range(refs):
-                ybuf[j] = jnp.dot(
-                    jnp.concatenate([xbuf[j], xbuf[j, :, 0 : 2 * LANES]], 1),
-                    y_mat[q, j],
-                    preferred_element_type=jnp.float32,
-                )
-            for w in range(windows):
-                width = min(STEP, width_all - w * STEP)
-                block = slice(w * rows, (w + 1) * rows)
-                for c in range(2):
-                    total = weights[0, block, 0:width] * ybuf[0, block, c * LANES : c * LANES + width]
-                    for j in range(1, refs):
-                        total = total + (
-                            weights[j, block, 0:width]
-                            * ybuf[j, block, c * LANES : c * LANES + width]
-                        )
-                    field[s, c, :, pl.ds(PAD + w * STEP, width)] = total
-
-            @pl.when(z < levels - 1)
-            def _():
-                send(s, 1 - slot)
-
+                        for n, (w, g) in enumerate(chosen):
+                            top = (j * 2 + c) * GROUP
+                            row = w * count + g * GROUP
+                            xbuf[
+                                j,
+                                row : row + GROUP,
+                                (p * 2 + c) * LANES : (p * 2 + c + 1) * LANES,
+                            ] = values[top : top + GROUP, n * LANES : (n + 1) * LANES]
+        before_write()
+        used = windows * count
+        for j in range(refs):
+            ybuf[j, 0:used] = jnp.dot(
+                jnp.concatenate([xbuf[j, 0:used], xbuf[j, 0:used, 0 : 2 * LANES]], 1),
+                y_mat[q, j],
+                preferred_element_type=jnp.float32,
+            )
+        for w in range(windows):
+            width = min(STEP, width_all - w * STEP)
+            block = slice(w * count, (w + 1) * count)
+            for c in range(2):
+                total = None
+                for j in range(refs):
+                    term = (
+                        weights[int(wide_step), j, block, 0:width]
+                        * ybuf[j, block, c * LANES : c * LANES + width]
+                    )
+                    total = term if total is None else total + term
+                target[s, c, :, pl.ds(PAD + w * STEP, width)] = total
+
+    def to_partner(z):
+        return pltpu.make_async_remote_copy(
+            src_ref=part.at[z],
+            dst_ref=inbox.at[lax.rem(z, far_levels)],
+            send_sem=part_sent.at[z],
+            recv_sem=inbox_sem.at[lax.rem(z, far_levels)],
+            device_id={"depth": partner},
+        )
+
+    def image_of(z, ref, from_row):
         mine = pl.ds(pl.multiple_of(PAD + side * (width_all - half), LANES), half)
+        taken = pl.ds(from_row, rows)
         total = jnp.zeros((rows, half), jnp.float32)
         for q in range(pairs):
-            total = total + field[2 * q, 0, :, mine] * field[2 * q + 1, 0, :, mine]
-            total = total - field[2 * q, 1, :, mine] * field[2 * q + 1, 1, :, mine]
+            total = total + ref[2 * q, 0, taken, mine] * ref[2 * q + 1, 0, taken, mine]
+            total = total - ref[2 * q, 1, taken, mine] * ref[2 * q + 1, 1, taken, mine]
 
         @pl.when(z // own_levels == me)
         def _():
@@ -340,12 +371,126 @@
         @pl.when(z // own_levels != me)
         def _():
             part[z] = total
+
+        @pl.when(jnp.logical_and(z // far_levels == side, z // own_levels != me))
+        def _():
             part_copy(z).start()
 
+        @pl.when(jnp.logical_and(z // far_levels != side, lax.rem(z, 2) != core))
+        def _():
+            to_partner(z).start()
+
+    def finish(z):
+        @pl.when(jnp.logical_and(z // far_levels != side, lax.rem(z, 2) == core))
+        def _():
+            to_partner(z).wait_recv()
+            part[z] = part[z] + inbox[lax.rem(z, far_levels)]
+            part_copy(z).start()
+
+    single = levels // 2
+
+    def one_level(z, carry):
+        slot = lax.rem(z, 2)
+
+        @pl.when(jnp.logical_and(core == 1, z < own_levels))
+        def _():
+            for a in range(2):
+                peer_table(True, a, z).start()
+
+        @pl.when(z + AHEAD < far_levels)
+        def _():
+            pass_on(z + AHEAD)
+
+        need(z)
+        set_weights(z, False)
+        for s in range(2 * pairs):
+            wait_arrived(s, slot, HALO)
+
+            def read_field(c, g, at):
+                if g == 0:
+                    return jnp.concatenate(
+                        [halo[slot, s, 0, c, FAR - HALO :, at], field[s, c, 0 : rows - HALO, at]], 0
+                    )
+                return jnp.concatenate(
+                    [field[s, c, HALO:rows, at], halo[slot, s, 1, c, 0:HALO, at]], 0
+                )
+
+            advance(s // 2, False, read_field, lambda: wait_sent(s, slot, HALO), field, s)
+
+            @pl.when(z < single - 1)
+            def _():
+                send(s, 1 - slot, HALO)
+
+            @pl.when(z == single - 1)
+            def _():
+                send(s, 1 - slot, FAR)
+
+        image_of(z, field, 0)
+
+        @pl.when(z > 0)
+        def _():
+            finish(z - 1)
+
         return carry
 
-    lax.fori_loop(0, levels, level, 0)
-
+    lax.fori_loop(0, single, one_level, 0)
+    need(single)
+    each_side(
+        lambda: rim_up(single // 2).start(), lambda: rim_down(single // 2).start()
+    )
+
+    def two_levels(h, carry):
+        slot = lax.rem(h, 2)
+        z = 2 * h
+        each_side(lambda: rim_down(h).wait_recv(), lambda: rim_up(h).wait_recv())
+        set_weights(z, True)
+        for s in range(2 * pairs):
+            wait_arrived(s, slot, FAR)
+
+            def read_wide(c, g, at):
+                if g == 0:
+                    return jnp.concatenate([halo[slot, s, 0, c, :, at], field[s, c, 0:FAR, at]], 0)
+                if g == 1:
+                    return field[s, c, :, at]
+                return jnp.concatenate(
+                    [field[s, c, rows - FAR : rows, at], halo[slot, s, 1, c, :, at]], 0
+                )
+
+            def read_middle(c, g, at):
+                return middle[s, c, g * GROUP : (g + 2) * GROUP, at]
+
+            advance(s // 2, True, read_wide, lambda: None, middle, s)
+            if s == 0:
+                need(z + 1)
+                set_weights(z + 1, False)
+            if s == 1:
+                @pl.when(z + 2 < levels)
+                def _():
+                    need(z + 2)
+                    each_side(lambda: rim_up(h + 1).start(), lambda: rim_down(h + 1).start())
+
+            advance(s // 2, False, read_middle, lambda: wait_sent(s, slot, FAR), field, s)
+
+            @pl.when(z + 2 < levels)
+            def _():
+                send(s, 1 - slot, FAR)
+
+        image_of(z, middle, HALO)
+        image_of(z + 1, field, 0)
+        finish(z - 1)
+
+        @pl.when(z > single)
+        def _():
+            finish(z - 2)
+
+        return carry
+
+    lax.fori_loop(single // 2, levels // 2, two_levels, 0)
+
+    finish(levels - 2)
+    finish(levels - 1)
+    for h in range(single // 2, levels // 2):
+        each_side(lambda: rim_up(h).wait_send(), lambda: rim_down(h).wait_send())
     for n in range(own_levels):
         for a in range(2):
             peer_table(False, a, n).wait_send()
@@ -363,16 +508,26 @@
     lax.fori_loop(0, levels, sent, 0)
     for n in range(own_levels):
         for d in range(depths):
-            @pl.when(d != me)
+            comes = jnp.logical_or(side == d // 2, d % 2 == n % 2)
+
+            @pl.when(jnp.logical_and(d != me, comes))
             def _():
                 pltpu.make_async_copy(
                     arrived.at[n, d], arrived.at[n, d], part_sem.at[n, d]
                 ).wait()
 
         for h in range(depths // 2):
-            image[n, :, h * half : (h + 1) * half] = (
-                arrived[n, 2 * h] + arrived[n, 2 * h + 1]
-            ) * (1.0 / (2 * pairs))
+            there = slice(h * half, (h + 1) * half)
+
+            @pl.when(side == h)
+            def _():
+                image[n, :, there] = (arrived[n, 2 * h] + arrived[n, 2 * h + 1]) * (
+                    1.0 / (2 * pairs)
+                )
+
+            @pl.when(side != h)
+            def _():
+                image[n, :, there] = arrived[n, 2 * h + n % 2] * (1.0 / (2 * pairs))
 
 
 def migrate(lat_size, depths, source, receiver, zone, blend, x_mat, y_mat):
@@ -394,21 +549,27 @@
         out_specs=vmem,
         scratch_shapes=[
             pltpu.VMEM((streams, 2, rows, wide), jnp.float32),
-            pltpu.VMEM((2, streams, 2, 2, HALO, wide), jnp.float32),
+            pltpu.VMEM((streams, 2, rows + 2 * HALO, wide), jnp.float32),
+            pltpu.VMEM((2, streams, 2, 2, FAR, wide), jnp.float32),
             pltpu.VMEM((2, levels, rows, width), jnp.int32),
-            pltpu.VMEM((refs, windows * rows, LANES), jnp.float32),
-            pltpu.VMEM((refs, windows * rows, 4 * LANES), jnp.bfloat16),
-            pltpu.VMEM((refs, windows * rows, 2 * LANES), jnp.float32),
+            pltpu.VMEM((levels // 2, 2, 2, HALO, width), jnp.int32),
+            pltpu.VMEM((2, refs, windows * (rows + 2 * HALO), LANES), jnp.float32),
+            pltpu.VMEM((refs, windows * (rows + 2 * HALO), 4 * LANES), jnp.bfloat16),
+            pltpu.VMEM((refs, windows * (rows + 2 * HALO), 2 * LANES), jnp.float32),
             pltpu.VMEM((levels, rows, half), jnp.float32),
+            pltpu.VMEM((2 * own_levels, rows, half), jnp.float32),
             pltpu.VMEM((own_levels, depths, rows, half), jnp.float32),
             dma((streams,)),
             dma((2, levels)),
             dma((2, 2, own_levels)),
             dma((2 * own_levels,)),
+            dma((levels // 2, 2)),
+            dma((levels // 2, 2)),
             dma((streams, 2)),
             dma((2, streams, 2)),
             dma((own_levels, depths)),
             dma((levels,)),
+            dma((2 * own_levels,)),
         ],
         compiler_params=pltpu.CompilerParams(
             collective_id=0, has_side_effects=True, vmem_limit_bytes=60 * 2**20

time: 130 us -> 125 us (0.962)
  Pallas kernels: 118 us -> 114 us
    pallas_call x1, Pallas kernels: 118 us -> 114 us  [migrate(): pl.pallas_call(functools.partial(body, lat_size), out_shape=jax.ShapeDtyp...]
where the time goes in v4:
time: 125 us
  Pallas kernels  114 us (91%)
  other arithmetic  6.34 us (5%)
  local copies, waits for them, and re-layouts  3.26 us (3%)
  between operations  1.55 us (1%)
    pallas_call x1, Pallas kernels, migrate(): pl.pallas_call(functools.partial(body, lat_size), out_shape=jax.ShapeDtyp...  114 us
    another operation x6, other arithmetic, local(): x_mat, y_mat = (jnp.stack(m) for m in zip(*made))  2.97 us

profile of v4, /device:TPU:97, one launch (start us, length us, event | category | flops | bytes accessed | tf_op | source)
XLA Modules:
  0.0 124.7 jit_solution(6188528851883246287)
XLA Ops:
  0.0 0.7 dynamic_slice.3
  0.7 0.6 fusion.50
  2.6 0.7 multiply_cosine_fusion.2
  3.4 0.1 fusion.31
  3.6 0.1 multiply_add_fusion.1
  3.7 0.2 fusion.12
  3.9 0.3 select_select_fusion.2
  4.2 0.3 select_select_fusion.3
  4.6 0.1 reduce-precision_convert_fusion.1
  4.7 0.1 maximum_bitcast_fusion
  4.8 0.3 select_select_fusion
  5.2 0.3 select_select_fusion.1
  5.5 0.2 reduce-precision_convert_fusion
  5.6 0.1 maximum_bitcast_fusion.1
  5.7 1.9 %pad_maximum_fusion.y_mat = bf16[2,4,768,256]{3,2,1,0:T(8,128)(2,1)} fusion(bf16[1,4,768,256]{3,2,1,0:T(8,128)(2,1)S(1)} %maximum_bitcast_fusion.1, bf16[1,4,768,256]{3,2,1,0:T(8,128)(2,1)S(1)} %maximum_bitcast_fusion), kind=kLoop, calls=%fused_computation | loop fusion | flops 1572864 | bytes 6291456 | tf_op jit(solution)/shard_map/stack | solution.py:586
  7.7 0.1 fusion.46
  7.8 0.1 select_select_fusion.7
  8.0 0.1 maximum_bitcast_fusion.2
  8.1 0.1 fusion.47
  8.3 0.1 select_select_fusion.5
  8.5 0.1 maximum_bitcast_fusion.3
  8.6 0.7 pad_maximum_fusion.1.x_mat
  9.3 113.5 %shard_map.64 = f32[4,32,1024]{2,1,0:T(8,128)} custom-call(f32[2,4,32,1024]{3,2,1,0:T(8,128)} %source.1, f32[2,4,32,1024]{3,2,1,0:T(8,128)} %receiver.1, s32[4,32,1024]{2,1,0:T(8,128)} %zone.1, s32[4,32,1024]{2,1,0:T(8,128)} %blend.1, bf16[2,128,192]{2,1,0:T(8,128)(2,1)} %pad_maximum_fusion.1.x_mat, bf16[2,4,768,256]{3,2,1,0:T(8,128)(2,1)} %pad_maximum_fusion.y_mat), custom_call_target="tpu_custom_call" | custom-call | tf_op jit(solution)/shard_map/pallas_call | solution.py:545
  122.8 1.9 %copy.8 = f32[4,32,1024]{2,1,0:T(8,128)} copy(f32[4,32,1024]{2,1,0:T(8,128)} %shard_map.64) | data formatting | bytes 1048576
  (21 shorter events, 0.4 us)

commit v5 on v4

--- a/solution.py
+++ b/solution.py
@@ -23,75 +23,79 @@
 taper_width = 16.0
 
 
-def kernels(frequency, ref_velocity):
-    offsets = jnp.arange(0, HALF + 1, dtype=jnp.int32).astype(jnp.float32)
-    wavenumber = 2.0 * math.pi * frequency.astype(jnp.float32) / ref_velocity
-    curvature = wavenumber * (cell_width * cell_width / (2.0 * depth_step))
-    phase_turn = wavenumber * depth_step
-    chirp_angle = curvature[:, None] * (offsets * offsets)[None, :]
-    envelope = jnp.exp(-offsets * offsets / taper_width)
-    raw_re = envelope * jnp.cos(chirp_angle)
-    raw_im = envelope * jnp.sin(chirp_angle)
-    both = jnp.where(offsets == 0.0, 1.0, 2.0)
-    magnitude = jnp.sqrt(
-        jnp.sum(both * raw_re, axis=-1) ** 2 + jnp.sum(both * raw_im, axis=-1) ** 2
-    )[:, None]
-    return raw_re / magnitude, raw_im / magnitude, jnp.cos(phase_turn), jnp.sin(phase_turn)
-
-
-def split(x):
-    high = lax.reduce_precision(x, 8, 7)
-    return high.astype(jnp.bfloat16), (x - high).astype(jnp.bfloat16)
-
-
-def banded(taps, distance, keep):
-    out = jnp.zeros((taps.shape[0],) + distance.shape, jnp.float32)
-    for m in range(HALF + 1):
-        out = jnp.where((distance == m) & keep, taps[:, m][:, None, None], out)
-    return out
-
-
-def matrices(frequency, ref_velocity):
-    c_re, c_im, turn_cos, turn_sin = kernels(frequency, ref_velocity)
-    refs = c_re.shape[0]
-    r = jnp.arange(GROUP)[:, None]
-    k = jnp.arange(2 * GROUP)[None, :]
-    distance = jnp.abs(k - HALO - r)
-    a_re, a_im = (banded(t, distance, True) for t in (c_re, c_im))
-    x_mat = jnp.concatenate(
-        [jnp.concatenate([a_re, -a_im], 2), jnp.concatenate([a_im, a_re], 2)], 1
-    ).reshape(refs * 2 * GROUP, 4 * GROUP)
-    x_high, x_low = split(x_mat)
-    x_all = jnp.concatenate([x_high, x_high, x_low], 1)
-    d_re = c_re * turn_cos[:, None] - c_im * turn_sin[:, None]
-    d_im = c_re * turn_sin[:, None] + c_im * turn_cos[:, None]
-    k = jnp.arange(LANES)[:, None]
-    n = jnp.arange(LANES)[None, :]
-    distance = jnp.abs(k - HALF - n)
-    b_re, b_im = (banded(t, distance, n < STEP) for t in (d_re, d_im))
-    y_mat = jnp.concatenate(
-        [jnp.concatenate([b_re, b_im], 2), jnp.concatenate([-b_im, b_re], 2)], 1
-    )
-    y_high, y_low = split(y_mat)
-    return x_all, jnp.concatenate([y_high, y_high, y_low], 1)
-
-
 def two_parts(x):
     high = x.astype(jnp.bfloat16)
     return high, (x - high.astype(jnp.float32)).astype(jnp.bfloat16)
 
 
+def taps_of(frequency, velocity):
+    shape = (8, LANES)
+    lane = lax.broadcasted_iota(jnp.int32, shape, 1)
+    wavenumber = jnp.full(shape, 2.0 * math.pi * frequency) / jnp.full(shape, velocity)
+    curvature = wavenumber * (cell_width * cell_width / (2.0 * depth_step))
+    phase_turn = wavenumber * depth_step
+    offset = jnp.minimum(lane, HALF + 1).astype(jnp.float32)
+    envelope = jnp.where(lane <= HALF, jnp.exp(-offset * offset / taper_width), 0.0)
+    angle = curvature * (offset * offset)
+    raw_re = envelope * jnp.cos(angle)
+    raw_im = envelope * jnp.sin(angle)
+    sides = jnp.where(lane == 0, 1.0, 2.0)
+    sum_re = jnp.sum(sides * raw_re, axis=1, keepdims=True)
+    sum_im = jnp.sum(sides * raw_im, axis=1, keepdims=True)
+    magnitude = jnp.sqrt(sum_re * sum_re + sum_im * sum_im)
+    c_re, c_im = raw_re / magnitude, raw_im / magnitude
+    turn_cos, turn_sin = jnp.cos(phase_turn), jnp.sin(phase_turn)
+    return c_re, c_im, c_re * turn_cos - c_im * turn_sin, c_re * turn_sin + c_im * turn_cos
+
+
+def banded(taps, distance):
+    out = jnp.zeros(distance.shape, jnp.float32)
+    for m in range(HALF + 1):
+        tap = jnp.broadcast_to(taps[0:1, m : m + 1], distance.shape)
+        out = jnp.where(distance == m, tap, out)
+    return out
+
+
+def set_matrices(at, frequency, velocity, x_mat, y_mat):
+    c_re, c_im, d_re, d_im = taps_of(frequency, velocity)
+    shape = (GROUP, 12 * GROUP)
+    lane = lax.broadcasted_iota(jnp.int32, shape, 1)
+    row = lax.broadcasted_iota(jnp.int32, shape, 0)
+    distance = jnp.abs(lax.rem(lane, 2 * GROUP) - HALO - row)
+    a_re, a_im = banded(c_re, distance), banded(c_im, distance)
+    from_re = lax.rem(lane, 4 * GROUP) < 2 * GROUP
+    for c, value in enumerate(
+        (jnp.where(from_re, a_re, -a_im), jnp.where(from_re, a_im, a_re))
+    ):
+        high = value.astype(jnp.bfloat16).astype(jnp.float32)
+        x_mat[at, c * GROUP : (c + 1) * GROUP] = jnp.where(
+            lane < 8 * GROUP, high, value - high
+        ).astype(jnp.bfloat16)
+    shape = (LANES, LANES)
+    k = lax.broadcasted_iota(jnp.int32, shape, 0)
+    n = lax.broadcasted_iota(jnp.int32, shape, 1)
+    distance = jnp.where(n < STEP, jnp.abs(k - HALF - n), 2 * LANES)
+    b_re, b_im = banded(d_re, distance), banded(d_im, distance)
+    for c, pair in enumerate(((b_re, b_im), (-b_im, b_re))):
+        for o, value in enumerate(pair):
+            for p, part in enumerate((0, 0, 1)):
+                y_mat[
+                    at,
+                    (2 * p + c) * LANES : (2 * p + c + 1) * LANES,
+                    o * LANES : (o + 1) * LANES,
+                ] = two_parts(value)[part]
+
+
 def body(
-    lat_size, source, receiver, zone, blend, x_mat, y_mat,
-    image, field, middle, halo, table, rim, weights, xbuf, ybuf, part, inbox, arrived,
+    lat_size, refs, source, receiver, zone, blend, velocities, frequencies,
+    image, x_mat, y_mat, field, middle, halo, table, rim, weights, xbuf, ybuf, part, inbox, arrived,
     load_sem, table_sem, table_sent, passed_sent, rim_sem, rim_sent,
     send_sem, recv_sem, part_sem, part_sent, inbox_sem,
 ):
     own_levels, rows, cols = zone.shape
     levels, width_all = table.shape[1], table.shape[3]
     depths = levels // own_levels
-    pairs = x_mat.shape[0]
-    refs = y_mat.shape[1]
+    pairs = y_mat.shape[0] // refs
     half = part.shape[2]
     windows = -(-width_all // STEP)
     lat = lax.axis_index("lat")
@@ -266,6 +270,18 @@
 
         for a in range(2):
             peer_table(False, a, n).start()
+
+    def prepare(at, carry):
+        set_matrices(
+            at,
+            frequencies[core * pairs + at // refs].astype(jnp.float32),
+            velocities[lax.rem(at, refs)],
+            x_mat,
+            y_mat,
+        )
+        return carry
+
+    lax.fori_loop(0, pairs * refs, prepare, 0)
     for i in range(AHEAD):
         pass_on(i)
 
@@ -311,7 +327,7 @@
                 parts.append(jnp.concatenate([read(c, g, at) for c in range(2)], 0))
             high, low = two_parts(jnp.concatenate(parts, 1))
             out = jnp.dot(
-                x_mat[q],
+                x_mat[q * refs : (q + 1) * refs].reshape(2 * refs * GROUP, 12 * GROUP),
                 jnp.concatenate([high, low, high], 0),
                 preferred_element_type=jnp.float32,
             )
@@ -331,7 +347,7 @@
         for j in range(refs):
             ybuf[j, 0:used] = jnp.dot(
                 jnp.concatenate([xbuf[j, 0:used], xbuf[j, 0:used, 0 : 2 * LANES]], 1),
-                y_mat[q, j],
+                y_mat[q * refs + j],
                 preferred_element_type=jnp.float32,
             )
         for w in range(windows):
@@ -387,7 +403,7 @@
             part[z] = part[z] + inbox[lax.rem(z, far_levels)]
             part_copy(z).start()
 
-    single = levels // 2
+    single = own_levels
 
     def one_level(z, carry):
         slot = lax.rem(z, 2)
@@ -463,6 +479,11 @@
             if s == 0:
                 need(z + 1)
                 set_weights(z + 1, False)
+            if s % 2 == 1:
+                @pl.when(z + s // 2 + AHEAD < far_levels)
+                def _():
+                    pass_on(z + s // 2 + AHEAD)
+
             if s == 1:
                 @pl.when(z + 2 < levels)
                 def _():
@@ -530,24 +551,28 @@
                 image[n, :, there] = arrived[n, 2 * h + n % 2] * (1.0 / (2 * pairs))
 
 
-def migrate(lat_size, depths, source, receiver, zone, blend, x_mat, y_mat):
+def migrate(lat_size, depths, source, receiver, zone, blend, velocities, frequencies):
     own_levels, rows, cols = zone.shape
     levels = depths * own_levels
-    pairs, refs = y_mat.shape[:2]
+    refs = velocities.shape[0]
+    pairs = frequencies.shape[0] // 2
     streams = 2 * pairs
     half = cols // 2
     width = half + -(-HALF * levels // LANES) * LANES
     windows = -(-width // STEP)
     vmem = pl.BlockSpec(memory_space=pltpu.VMEM)
+    smem = pl.BlockSpec(memory_space=pltpu.SMEM)
     hbm = pl.BlockSpec(memory_space=pl.ANY)
     wide = width + 2 * PAD
     dma = pltpu.SemaphoreType.DMA
     return pl.pallas_call(
-        functools.partial(body, lat_size),
+        functools.partial(body, lat_size, refs),
         out_shape=jax.ShapeDtypeStruct((own_levels, rows, cols), jnp.float32),
-        in_specs=[hbm, hbm, hbm, hbm, vmem, vmem],
+        in_specs=[hbm, hbm, hbm, hbm, smem, smem],
         out_specs=vmem,
         scratch_shapes=[
+            pltpu.VMEM((pairs * refs, 2 * GROUP, 12 * GROUP), jnp.bfloat16),
+            pltpu.VMEM((pairs * refs, 6 * LANES, 2 * LANES), jnp.bfloat16),
             pltpu.VMEM((streams, 2, rows, wide), jnp.float32),
             pltpu.VMEM((streams, 2, rows + 2 * HALO, wide), jnp.float32),
             pltpu.VMEM((2, streams, 2, 2, FAR, wide), jnp.float32),
@@ -574,18 +599,13 @@
         compiler_params=pltpu.CompilerParams(
             collective_id=0, has_side_effects=True, vmem_limit_bytes=60 * 2**20
         ),
-    )(source, receiver, zone, blend, x_mat, y_mat)
+    )(source, receiver, zone, blend, velocities, frequencies)
 
 
 def local(lat_size, source_field, receiver_field, zone_index, blend_weight, ref_velocity, frequencies):
-    depths = lax.axis_size("depth")
-    pairs = source_field.shape[1] // 2
-    core = lax.rem(lax.axis_index("depth"), 2)
-    chosen = lax.dynamic_slice_in_dim(frequencies, core * pairs, pairs)
-    made = [matrices(chosen[q], ref_velocity) for q in range(pairs)]
-    x_mat, y_mat = (jnp.stack(m) for m in zip(*made))
     return migrate(
-        lat_size, depths, source_field, receiver_field, zone_index, blend_weight, x_mat, y_mat
+        lat_size, lax.axis_size("depth"), source_field, receiver_field, zone_index,
+        blend_weight, ref_velocity, frequencies,
     )
 
 

time: 125 us -> 110 us (0.88)
  other arithmetic: 6.34 us -> 0 us
  Pallas kernels: 114 us -> 108 us
  between operations: 1.55 us -> 0.01 us
  local copies, waits for them, and re-layouts: 3.26 us -> 1.89 us
    pallas_call x1, Pallas kernels: 114 us -> 108 us  [migrate(): pl.pallas_call(functools.partial(body, lat_size, refs), out_shape=jax.Sha...]
    another operation x6 -> x0, other arithmetic: 2.97 us -> none  [local(): x_mat, y_mat = (jnp.stack(m) for m in zip(*made))]
    select_n x7 -> x0, other arithmetic: 1.41 us -> none  [the longest x6 1.4 us: banded(): out = jnp.where((distance == m) & keep, taps[:, m][:, None, None], out)]
where the time goes in v5:
time: 110 us
  Pallas kernels  108 us (98%)
  local copies, waits for them, and re-layouts  1.89 us (2%)
    pallas_call x1, Pallas kernels, migrate(): pl.pallas_call(functools.partial(body, lat_size, refs), out_shape=jax.Sha...  108 us

profile of v5, /device:TPU:97, one launch (start us, length us, event | category | flops | bytes accessed | tf_op | source)
XLA Modules:
  0.0 110.0 jit_solution(5784276072757712254)
XLA Ops:
  0.0 108.1 %shard_map.64 = f32[4,32,1024]{2,1,0:T(8,128)} custom-call(f32[2,4,32,1024]{3,2,1,0:T(8,128)} %source.1, f32[2,4,32,1024]{3,2,1,0:T(8,128)} %receiver.1, s32[4,32,1024]{2,1,0:T(8,128)} %zone.1, s32[4,32,1024]{2,1,0:T(8,128)} %blend.1, f32[4]{0:T(128)} %velocities.1, s32[4]{0:T(128)} %frequencies.1), custom_call_target="tpu_custom_call" | custom-call | tf_op jit(solution)/shard_map/pallas_call | solution.py:568
  108.1 1.9 %copy.8 = f32[4,32,1024]{2,1,0:T(8,128)} copy(f32[4,32,1024]{2,1,0:T(8,128)} %shard_map.64) | data formatting | bytes 1048576

commit v6 on v5

--- a/solution.py
+++ b/solution.py
@@ -315,17 +315,23 @@
                     which == j, lower, jnp.where(which == j - 1, upper, 0.0)
                 )
 
-    def advance(q, wide_step, read, before_write, target, s):
+    def advance(q, wide_step, read, before_write, target, streams):
         groups = 3 if wide_step else 2
         count = groups * GROUP
-        units = [(w, g) for w in range(windows) for g in range(groups)]
+        used = windows * count
+        split = {}
+        units = [(i, w, g) for i in range(len(streams)) for w in range(windows) for g in range(groups)]
         for first in range(0, len(units), 2):
             chosen = units[first : first + 2]
-            parts = []
-            for w, g in chosen:
-                at = pl.ds(PAD + w * STEP - HALF, LANES)
-                parts.append(jnp.concatenate([read(c, g, at) for c in range(2)], 0))
-            high, low = two_parts(jnp.concatenate(parts, 1))
+            highs, lows = [], []
+            for i, w, g in chosen:
+                if (i, w) not in split:
+                    at = pl.ds(PAD + w * STEP - HALF, LANES)
+                    split[i, w] = [two_parts(read(streams[i], c, at)) for c in range(2)]
+                taken = slice(g * GROUP, (g + 2) * GROUP)
+                highs.append(jnp.concatenate([both[0][taken] for both in split[i, w]], 0))
+                lows.append(jnp.concatenate([both[1][taken] for both in split[i, w]], 0))
+            high, low = jnp.concatenate(highs, 1), jnp.concatenate(lows, 1)
             out = jnp.dot(
                 x_mat[q * refs : (q + 1) * refs].reshape(2 * refs * GROUP, 12 * GROUP),
                 jnp.concatenate([high, low, high], 0),
@@ -334,34 +340,36 @@
             for p, values in enumerate(two_parts(out)):
                 for j in range(refs):
                     for c in range(2):
-                        for n, (w, g) in enumerate(chosen):
+                        for n, (i, w, g) in enumerate(chosen):
                             top = (j * 2 + c) * GROUP
-                            row = w * count + g * GROUP
+                            row = i * used + w * count + g * GROUP
                             xbuf[
                                 j,
                                 row : row + GROUP,
                                 (p * 2 + c) * LANES : (p * 2 + c + 1) * LANES,
                             ] = values[top : top + GROUP, n * LANES : (n + 1) * LANES]
         before_write()
-        used = windows * count
+        every = len(streams) * used
         for j in range(refs):
-            ybuf[j, 0:used] = jnp.dot(
-                jnp.concatenate([xbuf[j, 0:used], xbuf[j, 0:used, 0 : 2 * LANES]], 1),
+            ybuf[j, 0:every] = jnp.dot(
+                jnp.concatenate([xbuf[j, 0:every], xbuf[j, 0:every, 0 : 2 * LANES]], 1),
                 y_mat[q * refs + j],
                 preferred_element_type=jnp.float32,
             )
-        for w in range(windows):
-            width = min(STEP, width_all - w * STEP)
-            block = slice(w * count, (w + 1) * count)
-            for c in range(2):
-                total = None
-                for j in range(refs):
-                    term = (
-                        weights[int(wide_step), j, block, 0:width]
-                        * ybuf[j, block, c * LANES : c * LANES + width]
-                    )
-                    total = term if total is None else total + term
-                target[s, c, :, pl.ds(PAD + w * STEP, width)] = total
+        for i, s in enumerate(streams):
+            for w in range(windows):
+                width = min(STEP, width_all - w * STEP)
+                block = slice(w * count, (w + 1) * count)
+                made = slice(i * used + w * count, i * used + (w + 1) * count)
+                for c in range(2):
+                    total = None
+                    for j in range(refs):
+                        term = (
+                            weights[int(wide_step), j, block, 0:width]
+                            * ybuf[j, made, c * LANES : c * LANES + width]
+                        )
+                        total = term if total is None else total + term
+                    target[s, c, :, pl.ds(PAD + w * STEP, width)] = total
 
     def to_partner(z):
         return pltpu.make_async_remote_copy(
@@ -403,15 +411,16 @@
             part[z] = part[z] + inbox[lax.rem(z, far_levels)]
             part_copy(z).start()
 
-    single = own_levels
+    single = 2
 
     def one_level(z, carry):
         slot = lax.rem(z, 2)
 
-        @pl.when(jnp.logical_and(core == 1, z < own_levels))
-        def _():
-            for a in range(2):
-                peer_table(True, a, z).start()
+        @pl.when(jnp.logical_and(core == 1, 2 * z < own_levels))
+        def _():
+            for n in range(2):
+                for a in range(2):
+                    peer_table(True, a, 2 * z + n).start()
 
         @pl.when(z + AHEAD < far_levels)
         def _():
@@ -422,16 +431,17 @@
         for s in range(2 * pairs):
             wait_arrived(s, slot, HALO)
 
-            def read_field(c, g, at):
-                if g == 0:
-                    return jnp.concatenate(
-                        [halo[slot, s, 0, c, FAR - HALO :, at], field[s, c, 0 : rows - HALO, at]], 0
-                    )
+            def read_field(s, c, at):
                 return jnp.concatenate(
-                    [field[s, c, HALO:rows, at], halo[slot, s, 1, c, 0:HALO, at]], 0
+                    [
+                        halo[slot, s, 0, c, FAR - HALO :, at],
+                        field[s, c, :, at],
+                        halo[slot, s, 1, c, 0:HALO, at],
+                    ],
+                    0,
                 )
 
-            advance(s // 2, False, read_field, lambda: wait_sent(s, slot, HALO), field, s)
+            advance(s // 2, False, read_field, lambda: wait_sent(s, slot, HALO), field, [s])
 
             @pl.when(z < single - 1)
             def _():
@@ -456,45 +466,49 @@
     )
 
     def two_levels(h, carry):
-        slot = lax.rem(h, 2)
+        slot = lax.rem(h - single // 2, 2)
         z = 2 * h
         each_side(lambda: rim_down(h).wait_recv(), lambda: rim_up(h).wait_recv())
         set_weights(z, True)
-        for s in range(2 * pairs):
-            wait_arrived(s, slot, FAR)
-
-            def read_wide(c, g, at):
-                if g == 0:
-                    return jnp.concatenate([halo[slot, s, 0, c, :, at], field[s, c, 0:FAR, at]], 0)
-                if g == 1:
-                    return field[s, c, :, at]
-                return jnp.concatenate(
-                    [field[s, c, rows - FAR : rows, at], halo[slot, s, 1, c, :, at]], 0
-                )
-
-            def read_middle(c, g, at):
-                return middle[s, c, g * GROUP : (g + 2) * GROUP, at]
-
-            advance(s // 2, True, read_wide, lambda: None, middle, s)
-            if s == 0:
+
+        def read_wide(s, c, at):
+            return jnp.concatenate(
+                [halo[slot, s, 0, c, :, at], field[s, c, :, at], halo[slot, s, 1, c, :, at]], 0
+            )
+
+        def read_middle(s, c, at):
+            return middle[s, c, :, at]
+
+        for streams in ([0], [1], [2], [3]):
+            q = streams[0] // 2
+
+            def all_sent():
+                for s in streams:
+                    wait_sent(s, slot, FAR)
+
+            for s in streams:
+                wait_arrived(s, slot, FAR)
+            advance(q, True, read_wide, lambda: None, middle, streams)
+            if streams[0] == 0:
                 need(z + 1)
                 set_weights(z + 1, False)
-            if s % 2 == 1:
-                @pl.when(z + s // 2 + AHEAD < far_levels)
-                def _():
-                    pass_on(z + s // 2 + AHEAD)
-
-            if s == 1:
+                for ahead in range(AHEAD, 2 * AHEAD):
+                    @pl.when(z + ahead < far_levels)
+                    def _():
+                        pass_on(z + ahead)
+
+            if streams[-1] == 1:
                 @pl.when(z + 2 < levels)
                 def _():
                     need(z + 2)
                     each_side(lambda: rim_up(h + 1).start(), lambda: rim_down(h + 1).start())
 
-            advance(s // 2, False, read_middle, lambda: wait_sent(s, slot, FAR), field, s)
+            advance(q, False, read_middle, all_sent, field, streams)
 
             @pl.when(z + 2 < levels)
             def _():
-                send(s, 1 - slot, FAR)
+                for s in streams:
+                    send(s, 1 - slot, FAR)
 
         image_of(z, middle, HALO)
         image_of(z + 1, field, 0)
@@ -579,8 +593,8 @@
             pltpu.VMEM((2, levels, rows, width), jnp.int32),
             pltpu.VMEM((levels // 2, 2, 2, HALO, width), jnp.int32),
             pltpu.VMEM((2, refs, windows * (rows + 2 * HALO), LANES), jnp.float32),
-            pltpu.VMEM((refs, windows * (rows + 2 * HALO), 4 * LANES), jnp.bfloat16),
-            pltpu.VMEM((refs, windows * (rows + 2 * HALO), 2 * LANES), jnp.float32),
+            pltpu.VMEM((refs, 2 * windows * (rows + 2 * HALO), 4 * LANES), jnp.bfloat16),
+            pltpu.VMEM((refs, 2 * windows * (rows + 2 * HALO), 2 * LANES), jnp.float32),
             pltpu.VMEM((levels, rows, half), jnp.float32),
             pltpu.VMEM((2 * own_levels, rows, half), jnp.float32),
             pltpu.VMEM((own_levels, depths, rows, half), jnp.float32),

time: 110 us -> 108 us (0.982)
  Pallas kernels: 108 us -> 106 us
    pallas_call x1, Pallas kernels: 108 us -> 106 us  [migrate(): pl.pallas_call(functools.partial(body, lat_size, refs), out_shape=jax.Sha...]
where the time goes in v6:
time: 108 us
  Pallas kernels  106 us (98%)
  local copies, waits for them, and re-layouts  1.89 us (2%)
    pallas_call x1, Pallas kernels, migrate(): pl.pallas_call(functools.partial(body, lat_size, refs), out_shape=jax.Sha...  106 us

profile of v6, /device:TPU:97, one launch (start us, length us, event | category | flops | bytes accessed | tf_op | source)
XLA Modules:
  0.0 108.2 jit_solution(9054824089424701094)
XLA Ops:
  0.0 106.3 %shard_map.64 = f32[4,32,1024]{2,1,0:T(8,128)} custom-call(f32[2,4,32,1024]{3,2,1,0:T(8,128)} %source.1, f32[2,4,32,1024]{3,2,1,0:T(8,128)} %receiver.1, s32[4,32,1024]{2,1,0:T(8,128)} %zone.1, s32[4,32,1024]{2,1,0:T(8,128)} %blend.1, f32[4]{0:T(128)} %velocities.1, s32[4]{0:T(128)} %frequencies.1), custom_call_target="tpu_custom_call" | custom-call | tf_op jit(solution)/shard_map/pallas_call | solution.py:582
  106.3 1.9 %copy.8 = f32[4,32,1024]{2,1,0:T(8,128)} copy(f32[4,32,1024]{2,1,0:T(8,128)} %shard_map.64) | data formatting | bytes 1048576

commit v7 on v6

--- a/solution.py
+++ b/solution.py
@@ -428,6 +428,14 @@
 
         need(z)
         set_weights(z, False)
+
+        @pl.when(z == single - 1)
+        def _():
+            need(single)
+            each_side(
+                lambda: rim_up(single // 2).start(), lambda: rim_down(single // 2).start()
+            )
+
         for s in range(2 * pairs):
             wait_arrived(s, slot, HALO)
 
@@ -460,10 +468,6 @@
         return carry
 
     lax.fori_loop(0, single, one_level, 0)
-    need(single)
-    each_side(
-        lambda: rim_up(single // 2).start(), lambda: rim_down(single // 2).start()
-    )
 
     def two_levels(h, carry):
         slot = lax.rem(h - single // 2, 2)

time: 108 us -> 126 us (1.17)
  the two profiles are of different devices: /device:TPU:97 before, /device:TPU:127 now
where the time goes in v7:
time: 126 us
  Pallas kernels  124 us (98%)
  local copies, waits for them, and re-layouts  1.89 us (2%)
    pallas_call x1, Pallas kernels, migrate(): pl.pallas_call(functools.partial(body, lat_size, refs), out_shape=jax.Sha...  124 us

profile of v7, /device:TPU:127, one launch (start us, length us, event | category | flops | bytes accessed | tf_op | source)
XLA Modules:
  0.0 125.9 jit_solution(1291659327029081407)
XLA Ops:
  0.0 124.0 %shard_map.64 = f32[4,32,1024]{2,1,0:T(8,128)} custom-call(f32[2,4,32,1024]{3,2,1,0:T(8,128)} %source.1, f32[2,4,32,1024]{3,2,1,0:T(8,128)} %receiver.1, s32[4,32,1024]{2,1,0:T(8,128)} %zone.1, s32[4,32,1024]{2,1,0:T(8,128)} %blend.1, f32[4]{0:T(128)} %velocities.1, s32[4]{0:T(128)} %frequencies.1), custom_call_target="tpu_custom_call" | custom-call | tf_op jit(solution)/shard_map/pallas_call | solution.py:586
  124.0 1.9 %copy.8 = f32[4,32,1024]{2,1,0:T(8,128)} copy(f32[4,32,1024]{2,1,0:T(8,128)} %shard_map.64) | data formatting | bytes 1048576
